TPU v7x, 32 devices: a whole 2x2x4 slice. The times are simulated.
32 devices in a mesh: batch: 8 (over z, x), row: 2 (over y), col: 2 (over core).
Axes of the slice: x: 2, y: 2, z: 4, core: 2. Of those that a mesh axis runs over, the one named last changes fastest.
Arguments:
- basis_values: bfloat16 [32, 192, 2048], P(('batch', 'row', 'col')), may hold values from -6 to 6
- density_matrix: bfloat16 [32, 3, 192, 192], P(('batch', 'row', 'col')), may hold values from -0.03125 to 0.03125
- points: float32 [32, 3, 2048], P(('batch', 'row', 'col')), may hold values from -2 to 2
- weights: float32 [32, 2048], P(('batch', 'row', 'col')), may hold values from 0.128 to 1.28
- intersection: int32 [32, 32], P(('batch', 'row', 'col')), may hold values from 0 to 31, as said below
- basis_index: int32 [32, 192], P(('batch', 'row', 'col')), may hold values from 0 to 1535, as said below
- atom_positions: float32 [3, 32], replicated, may hold values from -2 to 2
- shell_blocks: int32 [32], replicated, may hold values from 1 to 8
- shell_widths: float32 [64], replicated, may hold values from 0.03125 to 0.0625
- green: bfloat16 [32, 8, 4096], P('batch'), may hold values from -0.0009765625 to 0.0009765625
Outputs:
- potential: bfloat16 [32, 12288], P('batch')
- hamiltonian: bfloat16 [3, 1536, 1536], P(None, 'row', 'col')
Inputs may be any that keep to these rules, and one draw needn't show every extreme that they name: `intersection`: within a batch the 32 atom numbers are distinct. The owner of atom a is a // 4; no owner holds more than 4 of one batch's atoms, and among the batches with equal row and col index one owner holds exactly 4 of the atoms of every such batch. `basis_index`: within a batch the numbers are distinct, and its q-th run of 96 entries lies in [q * 768, (q + 1) * 768).
All inputs are finite; a program needn't handle non-finite values.
Results may differ from a plain program's by a relative error of at most 0.0095.
Values may be sent and summed in bfloat16 or wider, within the bound.
No kernel may reach another device: no remote copies, remote signals or barrier semaphores. Data moves between devices by JAX's collectives and lax.ppermute only.
A program may use at most 128 MiB of HBM per device.

v0:
```python
import functools

import jax
import jax.numpy as jnp
from jax import lax
from jax.experimental import pallas as pl
from jax.experimental.pallas import tpu as pltpu
from jax.sharding import PartitionSpec as P


S = 64
DEG = 8
NB = 1536
LANES = 128
FAR = 1.0e6
LOG2E = 1.4426950408889634
NT = (((1,), (1,)), ((), ()))
SMEM = pl.BlockSpec(memory_space=pltpu.SMEM)
VMEM = pl.BlockSpec(memory_space=pltpu.VMEM)


def atom_finder(group, atoms_ref):
    if isinstance(group, int):
        return lambda i: atoms_ref[group + i]
    stride, row_flip, col_flip = group
    base = lax.axis_index("col") ^ col_flip
    if row_flip is not None:
        base = base + (lax.axis_index("row") ^ row_flip) * 2
    return lambda i: base + i * stride


def prepare(chosen, pos_ref, pts_ref, dist_ref, polar_ref, side_ref):
    count = len(chosen)
    rows = lax.broadcasted_iota(jnp.int32, (count, LANES), 0)
    centre = []
    for axis in range(3):
        column = jnp.zeros((count, LANES), jnp.float32)
        for k, atom in enumerate(chosen):
            column = jnp.where(rows == k, pos_ref[axis, atom], column)
        centre.append(column)
    for t in range(pts_ref.shape[2] // LANES):
        here = pl.ds(t * LANES, LANES)
        delta = [pts_ref[0, pl.ds(axis, 1), here] - centre[axis] for axis in range(3)]
        square = delta[0] * delta[0] + delta[1] * delta[1] + delta[2] * delta[2] + 0.01
        inverse = lax.rsqrt(square)
        dist_ref[t] = square * inverse
        for ladder, u in ((polar_ref, delta[2] * inverse), (side_ref, delta[0] * inverse)):
            older, old = jnp.ones_like(u), u
            ladder[t, pl.ds(0, count), :] = older
            ladder[t, pl.ds(count, count), :] = old
            for order in range(2, DEG):
                older, old = old, 2.0 * u * old - older
                ladder[t, pl.ds(order * count, count), :] = old


def prepare_shells(widths_ref, scale_ref):
    rows = lax.broadcasted_iota(jnp.int32, (8, LANES), 0)
    for start in range(0, S, 8):
        column = jnp.zeros((8, LANES), jnp.float32)
        for j in range(8):
            place = start + j
            shell = 2 * place if place < S // 2 else 2 * place - (S - 1)
            column = jnp.where(rows == j, widths_ref[shell], column)
        scale_ref[pl.ds(start, 8), :] = -LOG2E / (column * column)


def shell_columns(blocks, live, scale_ref):
    half = live // 2
    place = lax.broadcasted_iota(jnp.int32, (live, LANES), 0)
    shell = jnp.where(place < half, 2 * place, 2 * place - (live - 1))
    middle = jnp.where(shell < 8 * blocks, shell.astype(jnp.float32) * (4.0 / S), FAR)
    scale = jnp.concatenate(
        [scale_ref[pl.ds(0, half), :], scale_ref[pl.ds(S // 2, half), :]], axis=0
    )
    return middle, scale


def angular_tile(k, count, t, polar_ref, side_ref):
    side = side_ref[t, pl.ds(k, DEG, stride=count), :]
    return jnp.concatenate(
        [
            polar_ref[t, pl.ds(order * count + k, DEG, stride=0), :] * side
            for order in range(DEG)
        ],
        axis=0,
    ).astype(jnp.bfloat16)


def radial_tile(k, t, middle, scale, dist_ref):
    dist = dist_ref[t, pl.ds(k, 8, stride=0), :]
    gap = jnp.concatenate([dist] * (middle.shape[0] // 8), axis=0) - middle
    return jnp.exp2(gap * (gap * scale))


def moments_kernel(group, count, fresh, *refs):
    if fresh:
        (
            atoms_ref, pos_ref, blocks_ref, widths_ref, pts_ref, phi_ref, dens_ref, w_ref,
            out_ref, wd_ref, dist_ref, polar_ref, side_ref, scale_ref,
        ) = refs
    else:
        (
            atoms_ref, pos_ref, blocks_ref, widths_ref, pts_ref, wd_ref,
            out_ref, dist_ref, polar_ref, side_ref, scale_ref,
        ) = refs
    points = pts_ref.shape[2]
    if fresh:
        for start in range(0, points, 256):
            here = pl.ds(start, 256)
            phi = phi_ref[0, :, here]
            wide = phi.astype(jnp.float32)
            for c in range(3):
                product = jnp.dot(dens_ref[0, c], phi, preferred_element_type=jnp.float32)
                density = jnp.sum(wide * product, axis=0, keepdims=True)
                wd_ref[pl.ds(c, 1), here] = w_ref[:, here] * density
    atom_at = atom_finder(group, atoms_ref)
    prepare([atom_at(i) for i in range(count)], pos_ref, pts_ref, dist_ref, polar_ref, side_ref)
    prepare_shells(widths_ref, scale_ref)

    def body(k, carry):
        blocks = blocks_ref[atom_at(k)]

        live = S
        middle, scale = shell_columns(blocks, live, scale_ref)
        total = jnp.zeros((3 * live, S), jnp.float32)
        for start in range(0, points, 256):
            scaled, angles = [[], [], []], []
            for inner in (start, start + LANES):
                t = inner // LANES
                radial = radial_tile(k, t, middle, scale, dist_ref).astype(jnp.bfloat16)
                angles.append(angular_tile(k, count, t, polar_ref, side_ref))
                for c in range(3):
                    row = jnp.broadcast_to(wd_ref[pl.ds(c, 1), pl.ds(inner, LANES)], (16, LANES))
                    row = jnp.concatenate([row.astype(jnp.bfloat16)] * (live // 16), axis=0)
                    scaled[c].append(radial * row)
            left = jnp.concatenate([jnp.concatenate(s, axis=1) for s in scaled], axis=0)
            right = jnp.concatenate(angles, axis=1)
            total += lax.dot_general(left, right, NT, preferred_element_type=jnp.float32)
        half = live // 2
        for c in range(3):
            even = total[c * live : c * live + half]
            odd = total[c * live + half : (c + 1) * live]
            block = jnp.concatenate([even, odd], axis=1)
            if live < S:
                rest = jnp.zeros((S // 2 - half, LANES), jnp.float32)
                block = jnp.concatenate([block, rest], axis=0)
            out_ref[k, pl.ds(c * (S // 2), S // 2), :] = block.astype(out_ref.dtype)

        return carry

    lax.fori_loop(0, count, body, 0, unroll=8)


def table_scratch(count, points):
    tiles = points // LANES
    return [
        pltpu.VMEM((tiles, count, LANES), jnp.float32),
        pltpu.VMEM((tiles, DEG * count, LANES), jnp.float32),
        pltpu.VMEM((tiles, DEG * count, LANES), jnp.float32),
        pltpu.VMEM((S, LANES), jnp.float32),
    ]


def table_cost(count, points):
    cells = count * points * S
    return pl.CostEstimate(flops=cells * 3 * S * 2, bytes_accessed=cells, transcendentals=cells)


def moments_call(group, count, shared, wd=None, phi=None, dens=None, w=None):
    points = shared[-1].shape[2]
    fresh = wd is None
    out = [jax.ShapeDtypeStruct((count, 3 * S // 2, LANES), jnp.bfloat16)]
    args = list(shared)
    if fresh:
        out.append(jax.ShapeDtypeStruct((3, points), jnp.float32))
        args += [phi, dens, w]
    else:
        args += [wd]
    return pl.pallas_call(
        functools.partial(moments_kernel, group, count, fresh),
        out_shape=out,
        in_specs=[SMEM] * 4 + [VMEM] * (len(args) - 4),
        out_specs=[VMEM] * len(out),
        scratch_shapes=table_scratch(count, points),
        cost_estimate=table_cost(count, points),
        name="moments",
    )(*args)


def field_kernel(groups, size, carried, kept, last, *refs):
    (atoms_ref, pos_ref, blocks_ref, widths_ref, pts_ref), refs = refs[:5], refs[5:]
    tabs, refs = refs[: len(groups)], refs[len(groups) :]
    count = len(groups) * size
    if carried:
        acc_in, refs = refs[0], refs[1:]
    if last:
        (phi_ref, w_ref, marks_ref), outs, refs = refs[:3], refs[3:7], refs[7:]
    else:
        acc_ref, refs = refs[0], refs[1:]
    if kept:
        plane_ref, refs = refs[0], refs[1:]
        for order, tab in enumerate(tabs):
            plane_ref[order ^ lax.axis_index("col")] = tab[lax.axis_index("batch")]
    dist_ref, polar_ref, side_ref, scale_ref = refs[:4]
    if last:
        acc_ref, oper_ref = refs[4:]
    points = pts_ref.shape[2]
    finders = [atom_finder(group, atoms_ref) for group in groups]
    prepare([atom_at(i) for atom_at in finders for i in range(size)], pos_ref, pts_ref, dist_ref, polar_ref, side_ref)
    prepare_shells(widths_ref, scale_ref)
    acc_ref[...] = acc_in[...] if carried else jnp.zeros_like(acc_ref)

    def body(i, carry, tab_ref, atom_at, base):
        k = base + i
        blocks = blocks_ref[atom_at(i)]

        live, half = S, S // 2
        middle, scale = shell_columns(blocks, live, scale_ref)
        table = tab_ref[i].astype(jnp.float32)
        lines = []
        for c in range(3):
            block = table[c * (S // 2) : c * (S // 2) + half]
            lines += [block[:, :S], block[:, S:]]
        left = jnp.concatenate(lines, axis=0).astype(jnp.bfloat16)
        for start in range(0, points, 256):
            t = start // LANES
            right = jnp.concatenate(
                [angular_tile(k, count, t + d, polar_ref, side_ref) for d in range(2)], axis=1
            )
            spread = jnp.dot(left, right, preferred_element_type=jnp.float32)
            for d in range(2):
                here = pl.ds(start + d * LANES, LANES)
                radial = radial_tile(k, t + d, middle, scale, dist_ref)
                for c in range(3):
                    sums = acc_ref[pl.ds(8 * c, 8), here]
                    for r in range(0, live, 8):
                        at = c * live + r
                        sums += radial[r : r + 8] * spread[at : at + 8, d * LANES : (d + 1) * LANES]
                    acc_ref[pl.ds(8 * c, 8), here] = sums

        return carry

    for order, atom_at in enumerate(finders):
        step = functools.partial(body, tab_ref=tabs[order], atom_at=atom_at, base=order * size)
        lax.fori_loop(0, size, step, 0, unroll=4)
    if last:
        piece = phi_ref.shape[1] // 2
        third = piece // 3
        sides = (lax.axis_index("row"), lax.axis_index("col"))
        halves = [[flip ^ side for flip in range(2)] for side in sides]
        spans = [[pl.ds(pl.multiple_of(h * piece, 32), piece) for h in pair] for pair in halves]
        quads = {}
        for c in range(3):
            for start in range(0, points, 256):
                here = pl.ds(start, 256)
                total = jnp.sum(acc_ref[pl.ds(8 * c, 8), here], axis=0, keepdims=True)
                wide = phi_ref[0, :, here].astype(jnp.float32)
                oper_ref[:, here] = (wide * (w_ref[:, here] * total)).astype(jnp.bfloat16)
            for x in range(2):
                for y in range(2):
                    quads[c, x, y] = lax.dot_general(
                        oper_ref[spans[0][x], :],
                        phi_ref[0, spans[1][y], :],
                        NT,
                        preferred_element_type=jnp.float32,
                    )
        for x in range(2):
            for y in range(2):
                q0, q1, q2 = (quads[c, x, y] for c in range(3))
                marks = [marks_ref[halves[0][x]], marks_ref[halves[1][y]]]
                marks = jnp.concatenate(marks + [jnp.zeros((third - 16, third), jnp.float32)], axis=0)
                parts = [q2[b * third : (b + 1) * third, 2 * third :] for b in range(3)] + [marks]
                blocks = [
                    jnp.concatenate([q0, q2[:, :third]], axis=1),
                    jnp.concatenate([q1, q2[:, third : 2 * third]], axis=1),
                    jnp.concatenate(parts, axis=1),
                ]
                outs[2 * y + x][0] = jnp.concatenate(blocks, axis=0).astype(jnp.bfloat16)


def field_call(groups, size, shared, tables, acc=None, keep=True, ends=None):
    points = shared[-1].shape[2]
    last = ends is not None
    count = len(groups) * size
    args = list(shared) + list(tables) + ([] if acc is None else [acc])
    scratch = table_scratch(count, points)
    if last:
        args += ends
        third = ends[0].shape[1] // 6
        out = [jax.ShapeDtypeStruct((1, 7 * third, LANES), jnp.bfloat16)] * 4
        scratch += [pltpu.VMEM((24, points), jnp.float32), pltpu.VMEM(ends[0].shape[1:], jnp.bfloat16)]
    else:
        out = [jax.ShapeDtypeStruct((24, points), jnp.float32)]
    if keep:
        out.append(jax.ShapeDtypeStruct((len(groups),) + tables[0].shape[1:], jnp.bfloat16))
    return pl.pallas_call(
        functools.partial(field_kernel, groups, size, acc is not None, keep, last),
        out_shape=out,
        in_specs=[SMEM] * 4 + [VMEM] * (len(args) - 4),
        out_specs=[VMEM] * len(out),
        scratch_shapes=scratch,
        cost_estimate=table_cost(count, points),
        name="field",
    )(*args)


def place_kernel(pieces, carried, final, piece, tile, *refs):
    stacks, refs = refs[:pieces], refs[pieces:]
    if carried:
        acc_in, refs = refs[0], refs[1:]
    out_ref, rows_ref, wide_ref = refs[:3]
    if final:
        hold_ref, sem_ref = refs[3:]
    third = piece // 3
    group = 4
    total = rows_ref.shape[1] // piece
    lane = lax.broadcasted_iota(jnp.int32, (piece, LANES), 1).astype(jnp.int16)
    sub = lax.broadcasted_iota(jnp.int32, (tile, LANES), 0).astype(jnp.int16)
    one, zero = jnp.bfloat16(1), jnp.bfloat16(0)
    per = total // pieces
    for first in range(0, total, group):
        strips = []
        for g in range(first, first + group):
            ref, at = stacks[g // per], g % per
            tail = ref[at, pl.ds(2 * piece, third), :].astype(jnp.float32)
            marks = tail[: third // 2, 3 * third :]
            row_mark = marks[0:3] * 32.0 + marks[3:6]
            col_mark = marks[8:11] * 32.0 + marks[11:14]
            strips += [row_mark[b : b + 1] for b in range(3)]
            flat = jnp.concatenate([col_mark[b : b + 1] for b in range(3)] + [col_mark[0:1]], axis=1)
            column = jnp.transpose(jnp.broadcast_to(flat, (LANES, LANES)))[:piece].astype(jnp.int32).astype(jnp.int16)
            hits = jnp.concatenate(
                [
                    jnp.where(column == lane + u, one, zero)
                    for u in range(0, tile, LANES)
                ],
                axis=1,
            )
            upper = ref[at, pl.ds(0, piece), :].astype(jnp.float32)
            lower = ref[at, pl.ds(piece, piece), :].astype(jnp.float32)
            rest = jnp.concatenate([tail[:, b * third : (b + 1) * third] for b in range(3)], axis=0)
            shared = jnp.concatenate([upper[:, piece:], lower[:, piece:], rest], axis=1)
            quads = jnp.concatenate([upper[:, :piece], lower[:, :piece], shared], axis=0)
            spread = jnp.dot(
                quads.astype(jnp.bfloat16), hits, preferred_element_type=jnp.float32
            ).astype(jnp.bfloat16)
            for c in range(3):
                wide_ref[c, pl.ds(g * piece, piece), :] = spread[c * piece : (c + 1) * piece]
        strip = jnp.concatenate(strips, axis=1).astype(jnp.int32)
        strip = jnp.broadcast_to(strip, (16, strip.shape[1])).astype(jnp.int16)
        strip = jnp.concatenate([strip] * (tile // 16), axis=0)
        for start in range(0, group * piece, LANES):
            rows_ref[:, pl.ds(first * piece + start, LANES)] = (
                jnp.where(sub == strip[:, start : start + LANES], one, zero)
            )

    copies = []
    for c in range(3):
        value = jnp.dot(rows_ref[...], wide_ref[c], preferred_element_type=jnp.float32)
        if carried:
            value += acc_in[c]
        if final:
            hold_ref[c] = value.astype(out_ref.dtype)
            copies.append(pltpu.make_async_copy(hold_ref.at[c], out_ref.at[c], sem_ref.at[c]))
            copies[-1].start()
        else:
            out_ref[c] = value
    for copy in copies:
        copy.wait()


def place_call(stacks, piece, tile, acc=None, final=True):
    total = sum(stack.shape[0] for stack in stacks)
    depth = total * piece
    args = list(stacks) + ([] if acc is None else [acc])
    return pl.pallas_call(
        functools.partial(place_kernel, len(stacks), acc is not None, final, piece, tile),
        out_shape=jax.ShapeDtypeStruct((3, tile, tile), jnp.bfloat16 if final else jnp.float32),
        in_specs=[VMEM] * len(args),
        out_specs=pl.BlockSpec(memory_space=pl.ANY) if final else VMEM,
        scratch_shapes=[
            pltpu.VMEM((tile, depth), jnp.bfloat16),
            pltpu.VMEM((3, depth, tile), jnp.bfloat16),
        ]
        + ([pltpu.VMEM((3, tile, tile), jnp.bfloat16), pltpu.SemaphoreType.DMA((3,))] if final else []),
        input_output_aliases={} if acc is None or final else {len(stacks): 0},
        compiler_params=pltpu.CompilerParams(vmem_limit_bytes=28 << 20),
        cost_estimate=pl.CostEstimate(
            flops=8 * 3 * depth * tile * tile, bytes_accessed=12 * tile * tile, transcendentals=0
        ),
        name="place",
    )(*args)


def apply_green(charges, kernels):
    shaped = charges.astype(jnp.bfloat16).reshape(-1, 3, S, DEG, DEG)
    kernel_rows = kernels.reshape(-1, DEG, S, S)
    result = jnp.einsum(
        "xast,xctam->xcsam", kernel_rows, shaped, preferred_element_type=jnp.float32
    )
    return result.astype(jnp.bfloat16).reshape(-1, 3 * S * DEG * DEG)


def swap(value, axis, mask=1):
    size = lax.axis_size(axis)
    return lax.ppermute(value, axis, [(i, i ^ mask) for i in range(size)])


def on_device(
    basis_values,
    density_matrix,
    points,
    weights,
    intersection,
    basis_index,
    atom_positions,
    shell_blocks,
    shell_widths,
    green,
):
    atoms = intersection[0]
    labels = basis_index[0]
    owners = lax.axis_size("batch")
    parts = lax.axis_size("row")
    sides = lax.axis_size("col")
    row, col = lax.axis_index("row"), lax.axis_index("col")
    count = atoms.shape[0]
    slots = (count + owners - 1) // owners
    holding = green.shape[0]
    every_atom = atom_positions.shape[1]
    width = 3 * S * DEG * DEG
    lines = width // LANES
    highest = lax.Precision.HIGHEST
    dense = count == every_atom and holding == parts * sides
    plane = ("row", "col")
    across = [(i, i ^ 3) for i in range(parts * sides)]
    half, group = count // 2, count // 4
    shared = (atoms, atom_positions, shell_blocks, shell_widths, points)
    wanted = ((sides, None, 0), (sides, None, 1)) if dense else (0, half)
    listed = [(holding, f & 1, f >> 1) if dense else f * group for f in range(4)]
    other, weighted = moments_call(
        wanted[1], half, shared, phi=basis_values, dens=density_matrix, w=weights
    )
    mate = swap(other, "col") if dense else other
    first = moments_call(wanted[0], half, shared, wd=weighted)[0]
    if dense:
        held = first + mate
        shares = lax.all_to_all(held, ("batch", "row"), split_axis=0, concat_axis=0, tiled=True)
        charges = jnp.sum(shares.astype(jnp.float32), axis=0)
        kernels = lax.dynamic_index_in_dim(green, row * sides + col, 0, keepdims=True)
        mine = apply_green(charges.reshape(1, width), kernels).reshape(1, lines, LANES)
        own = lax.all_to_all(
            jnp.broadcast_to(mine, (owners, lines, LANES)),
            "batch",
            split_axis=0,
            concat_axis=0,
            tiled=True,
        )
        beside = swap(own, "row")
        beyond = lax.ppermute(own, plane, across)
        tables = [own, beside, swap(own, "col"), beyond]
    else:
        moments = jnp.concatenate([first, other])
        moments = moments.astype(jnp.float32).reshape(count, width)
        home = atoms // holding
        local_slot = atoms % holding
        order = jnp.arange(count)
        before = (home[None, :] == home[:, None]) & (order[None, :] < order[:, None])
        place = home * slots + jnp.sum(before, axis=1)
        routing = jnp.arange(owners * slots)[:, None] == place[None, :]
        outgoing = jnp.dot(routing.astype(jnp.float32), moments, precision=highest).reshape(
            owners, slots, width
        )
        tags = (jnp.sum(jnp.where(routing, local_slot[None, :] + 1, 0), axis=1) - 1).reshape(
            owners, slots
        )
        incoming, sources = (
            lax.all_to_all(outgoing, "batch", split_axis=0, concat_axis=0, tiled=True),
            lax.all_to_all(tags, "batch", split_axis=0, concat_axis=0, tiled=True),
        )
        collect = jnp.arange(holding)[:, None] == sources.reshape(1, owners * slots)
        partial_value = jnp.dot(
            collect.astype(jnp.float32), incoming.reshape(owners * slots, width), precision=highest
        )
        totals = lax.psum(partial_value, ("row", "col"))
        potential = apply_green(totals, green)
        back = jnp.dot(
            collect.T.astype(jnp.bfloat16), potential, preferred_element_type=jnp.float32
        ).astype(jnp.bfloat16)
        returned = lax.all_to_all(
            back.reshape(owners, slots, width), "batch", split_axis=0, concat_axis=0, tiled=True
        )
        table = jnp.dot(
            routing.T.astype(jnp.bfloat16),
            returned.reshape(owners * slots, width),
            preferred_element_type=jnp.float32,
        )
        table = table.astype(jnp.bfloat16).reshape(count, lines, LANES)
        tables = [table[place * group : (place + 1) * group] for place in range(4)]
    piece = labels.shape[0] // parts
    tile = NB // parts
    inner = labels.reshape(parts, 3, piece // 3) - jnp.arange(parts)[:, None, None] * tile
    marks = jnp.concatenate([inner // 32, inner % 32, inner[:, :2] * 0], axis=1)
    marks = marks.astype(jnp.float32)
    ends = [basis_values, weights, marks]
    spread = functools.partial(field_call, size=group, shared=shared, keep=dense)
    field, *ours = spread((listed[0], listed[2]), tables=[tables[0], tables[2]])
    load = spread((listed[1], listed[3]), tables=[tables[1], tables[3]], acc=field, ends=ends)
    if dense:
        ours, theirs = ours[0], load[4]
        potential = jnp.concatenate(
            [jnp.where(row == 0, ours, theirs), jnp.where(row == 0, theirs, ours)]
        ).reshape(holding, width)
    got = [swap(load[2], "col"), swap(load[1], "row"), lax.ppermute(load[3], plane, across)]
    plane_load = jnp.concatenate([load[0]] + got, axis=0)
    if owners <= 8:
        near, far = [plane_load], []
        for step in range(2, owners, 2):
            near.append(swap(plane_load, "batch", step))
        for line in near:
            far.append(swap(line, "batch"))
        stages = [near[:1]] + [list(pair) for pair in zip(near[1:], far)] + [far[-1:]]
        total = None
        for order, lines in enumerate(stages):
            total = place_call(lines, piece, tile, total, final=lines is stages[-1])
        hamiltonian = total
    else:
        everyone = lax.all_gather(plane_load, "batch", axis=0)
        chunk = 2
        everyone = everyone.reshape((owners // chunk, chunk * 4) + plane_load.shape[1:])

        def add(total, item):
            return place_call([item], piece, tile, total, final=False), None

        total, _ = lax.scan(add, jnp.zeros((3, tile, tile), jnp.float32), everyone)
        hamiltonian = total.astype(jnp.bfloat16)
    return (potential, hamiltonian)


def solution(mesh):
    return jax.shard_map(
        on_device,
        mesh=mesh,
        in_specs=(
            P(("batch", "row", "col"), None, None),
            P(("batch", "row", "col"), None, None, None),
            P(("batch", "row", "col"), None, None),
            P(("batch", "row", "col"), None),
            P(("batch", "row", "col"), None),
            P(("batch", "row", "col"), None),
            P(),
            P(),
            P(),
            P("batch", None, None),
        ),
        out_specs=(P("batch", None), P(None, "row", "col")),
        check_vma=False,
    )
```

profile of v0, /device:TPU:0, one launch (start us, length us, event | category | flops | bytes accessed | tf_op | source)
XLA Modules:
  0.0 116.9 jit_solution(2072604901290826661)
XLA Ops:
  0.7 1.4 %copy.23.refs_4_ = f32[1,3,2048]{2,1,0:T(4,128)} copy(f32[1,3,2048]{2,0,1:T(1,128)} %param.12) | data formatting | bytes 49152 | tf_op args[2]
  2.1 6.8 %moments.2 = (bf16[16,96,128]{2,1,0:T(8,128)(2,1)}, f32[3,2048]{1,0:T(4,128)}) custom-call(s32[32]{0:T(128)} %bitcast.16, f32[3,32]{1,0:T(4,128)} %refs_1_.7, s32[32]{0:T(128)} %refs_2_.7, f32[64]{0:T(128)} %refs_3_.7, f32[1,3,2048]{2,1,0:T(4,128)} %copy.23.refs_4_, bf16[1,192,2048]{2,1,0:T(8,128)(2,1)} %refs_8_.1, bf16[1,3,192,192]{3,2,1,0:T(8,128)(2,1)} %refs_6_.1, ...), custom_call_target="tpu_custom_call" | custom-call | flops 805306368 | bytes 2097152 | tf_op jit(solution)/shard_map/moments/pallas_call | solution.py:179
  9.4 5.5 %moments.3 = bf16[16,96,128]{2,1,0:T(8,128)(2,1)} custom-call(s32[32]{0:T(128)} %bitcast.17, f32[3,32]{1,0:T(4,128)} %refs_1_.7, s32[32]{0:T(128)} %refs_2_.7, f32[64]{0:T(128)} %refs_3_.7, f32[1,3,2048]{2,1,0:T(4,128)} %copy.23.refs_4_, f32[3,2048]{1,0:T(4,128)} %get-tuple-element.11.refs_5_), custom_call_target="tpu_custom_call" | custom-call | flops 805306368 | bytes 2097152 | tf_op jit(solution)/shard_map/moments/pallas_call | solution.py:179
  14.9 1.8 %add.17 = bf16[16,96,128]{2,1,0:T(8,128)(2,1)} add(bf16[16,96,128]{2,1,0:T(8,128)(2,1)} %moments.3, bf16[16,96,128]{2,1,0:T(8,128)(2,1)S(1)} %collective-permute-done) | non-fusion elementwise | flops 196608 | bytes 1179648 | tf_op jit(solution)/shard_map/add | solution.py:447
  16.8 7.8 %all-to-all-start = ((bf16[16,96,128]{2,1,0:T(8,128)(2,1)}), bf16[16,96,128]{2,1,0:T(8,128)(2,1)S(1)}, u32[]{:S(2)}, u32[]{:S(2)}) async-start(bf16[16,96,128]{2,1,0:T(8,128)(2,1)} %add.17), calls=%async_computation | async-start | bytes 786432 | tf_op jit(solution)/shard_map/all_to_all | solution.py:448
  24.8 13.0 %all-to-all-done = bf16[16,96,128]{2,1,0:T(8,128)(2,1)S(1)} async-done(((bf16[16,96,128]{2,1,0:T(8,128)(2,1)}), bf16[16,96,128]{2,1,0:T(8,128)(2,1)S(1)}, u32[]{:S(2)}, u32[]{:S(2)}) %all-to-all-start) | async-done | bytes 393248 | tf_op jit(solution)/shard_map/all_to_all | solution.py:448
  40.0 3.6 %all-to-all-start.1 = ((bf16[8,96,128]{2,1,0:T(8,128)(2,1)}), bf16[8,96,128]{2,1,0:T(8,128)(2,1)S(1)}, u32[]{:S(2)}, u32[]{:S(2)}) async-start(bf16[8,96,128]{2,1,0:T(8,128)(2,1)} %broadcast_in_dim.9), calls=%async_computation.1 | async-start | bytes 393216 | tf_op jit(solution)/shard_map/all_to_all | solution.py:452
  45.0 6.3 %all-to-all-done.1.refs_5_ = bf16[8,96,128]{2,1,0:T(8,128)(2,1)S(1)} async-done(((bf16[8,96,128]{2,1,0:T(8,128)(2,1)}), bf16[8,96,128]{2,1,0:T(8,128)(2,1)S(1)}, u32[]{:S(2)}, u32[]{:S(2)}) %all-to-all-start.1) | async-done | bytes 196640 | tf_op jit(solution)/shard_map/all_to_all | solution.py:452
  51.9 1.3 %collective-permute-start.3 = (bf16[8,96,128]{2,1,0:T(8,128)(2,1)S(1)}, bf16[8,96,128]{2,1,0:T(8,128)(2,1)S(1)}, u32[]{:S(2)}, u32[]{:S(2)}) collective-permute-start(bf16[8,96,128]{2,1,0:T(8,128)(2,1)S(1)} %all-to-all-done.1.refs_5_), channel_id=1, source_target_pairs={{0,3},{1,2},{2,1},{3,0},{4,7},{5,6},{6,5},{7,4},{8,11},{9,10},{10,... | collective-permute-start | bytes 589832 | tf_op jit(solution)/shard_map/ppermute | solution.py:460
  54.6 6.2 %field.2 = (f32[24,2048]{1,0:T(8,128)}, bf16[2,96,128]{2,1,0:T(8,128)(2,1)}) custom-call(s32[32]{0:T(128)} %bitcast.18, f32[3,32]{1,0:T(4,128)} %refs_1_.7, s32[32]{0:T(128)} %refs_2_.7, f32[64]{0:T(128)} %refs_3_.7, f32[1,3,2048]{2,1,0:T(4,128)} %copy.23.refs_4_, bf16[8,96,128]{2,1,0:T(8,128)(2,1)} %copy-done.1, bf16[8,96,128]{2,1,0:T(8,128)(2,1)} %copy-done.5), custom_call_target="tpu_custom_call" | custom-call | flops 805306368 | bytes 2097152 | tf_op jit(solution)/shard_map/field/pallas_call | solution.py:296
  60.8 1.6 %collective-permute-done.3.refs_6_ = bf16[8,96,128]{2,1,0:T(8,128)(2,1)S(1)} collective-permute-done((bf16[8,96,128]{2,1,0:T(8,128)(2,1)S(1)}, bf16[8,96,128]{2,1,0:T(8,128)(2,1)S(1)}, u32[]{:S(2)}, u32[]{:S(2)}) %collective-permute-start.3) | collective-permute-done | bytes 196640 | tf_op jit(solution)/shard_map/ppermute | solution.py:460
  63.1 8.5 %field.3 = (bf16[1,224,128]{2,1,0:T(8,128)(2,1)}, bf16[1,224,128]{2,1,0:T(8,128)(2,1)}, bf16[1,224,128]{2,1,0:T(8,128)(2,1)}, bf16[1,224,128]{2,1,0:T(8,128)(2,1)}, bf16[2,96,128]{2,1,0:T(8,128)(2,1)}) custom-call(s32[32]{0:T(128)} %bitcast.19, f32[3,32]{1,0:T(4,128)} %refs_1_.7, s32[32]{0:T(128)} %refs_2_.7, f32[64]{0:T(128)} %refs_3_.7, ...), custom_call_target="tpu_custom_call" | custom-call | flops 805306368 | bytes 2097152 | tf_op jit(solution)/shard_map/field/pallas_call | solution.py:296
  75.9 1.0 collective-permute-done.5
  77.1 1.2 %collective-permute-start.13 = (bf16[4,224,128]{2,1,0:T(8,128)(2,1)S(1)}, bf16[4,224,128]{2,1,0:T(8,128)(2,1)S(1)}, u32[]{:S(2)}, u32[]{:S(2)}) collective-permute-start(bf16[4,224,128]{2,1,0:T(8,128)(2,1)S(1)} %constant_dynamic-update-slice_fusion.refs_0_), channel_id=1, source_target_pairs={{0,4},{4,0},{8,12},{12,8},{16,20},{20,16},{24,28},{28,24},{1,5},{5... | collective-permute-start | bytes 688136 | tf_op jit(solution)/shard_map/ppermute | solution.py:406
  78.4 1.2 %collective-permute-start.9 = (bf16[4,224,128]{2,1,0:T(8,128)(2,1)S(1)}, bf16[4,224,128]{2,1,0:T(8,128)(2,1)S(1)}, u32[]{:S(2)}, u32[]{:S(2)}) collective-permute-start(bf16[4,224,128]{2,1,0:T(8,128)(2,1)S(1)} %constant_dynamic-update-slice_fusion.refs_0_), channel_id=1, source_target_pairs={{0,16},{4,20},{8,24},{12,28},{16,0},{20,4},{24,8},{28,12},{1,17},{... | collective-permute-start | bytes 688136 | tf_op jit(solution)/shard_map/ppermute | solution.py:406
  79.6 2.7 %collective-permute-start.7 = (bf16[4,224,128]{2,1,0:T(8,128)(2,1)S(1)}, bf16[4,224,128]{2,1,0:T(8,128)(2,1)S(1)}, u32[]{:S(2)}, u32[]{:S(2)}) collective-permute-start(bf16[4,224,128]{2,1,0:T(8,128)(2,1)S(1)} %constant_dynamic-update-slice_fusion.refs_0_), channel_id=1, source_target_pairs={{0,24},{4,28},{8,16},{12,20},{16,8},{20,12},{24,0},{28,4},{1,25},{... | collective-permute-start | bytes 688136 | tf_op jit(solution)/shard_map/ppermute | solution.py:406
  82.3 2.6 %place.5.refs_2_ = f32[3,768,768]{2,1,0:T(8,128)S(1)} custom-call(bf16[4,224,128]{2,1,0:T(8,128)(2,1)S(1)} %constant_dynamic-update-slice_fusion.refs_0_), custom_call_target="tpu_custom_call" | custom-call | flops 5435817984 | bytes 7077888 | tf_op jit(solution)/shard_map/place/pallas_call | solution.py:376
  85.0 3.2 %collective-permute-done.11.refs_0_ = bf16[4,224,128]{2,1,0:T(8,128)(2,1)S(1)} collective-permute-done((bf16[4,224,128]{2,1,0:T(8,128)(2,1)S(1)}, bf16[4,224,128]{2,1,0:T(8,128)(2,1)S(1)}, u32[]{:S(2)}, u32[]{:S(2)}) %collective-permute-start.11) | collective-permute-done | bytes 229408 | tf_op jit(solution)/shard_map/ppermute | solution.py:406
  88.3 9.3 %collective-permute-done.9.refs_0_ = bf16[4,224,128]{2,1,0:T(8,128)(2,1)S(1)} collective-permute-done((bf16[4,224,128]{2,1,0:T(8,128)(2,1)S(1)}, bf16[4,224,128]{2,1,0:T(8,128)(2,1)S(1)}, u32[]{:S(2)}, u32[]{:S(2)}) %collective-permute-start.9) | collective-permute-done | bytes 229408 | tf_op jit(solution)/shard_map/ppermute | solution.py:406
  98.4 1.2 %collective-permute-start.8 = (bf16[4,224,128]{2,1,0:T(8,128)(2,1)S(1)}, bf16[4,224,128]{2,1,0:T(8,128)(2,1)S(1)}, u32[]{:S(2)}, u32[]{:S(2)}) collective-permute-start(bf16[4,224,128]{2,1,0:T(8,128)(2,1)S(1)} %collective-permute-done.7.refs_0_), channel_id=1, source_target_pairs={{0,4},{4,0},{8,12},{12,8},{16,20},{20,16},{24,28},{28,24},{1,5},{5... | collective-permute-start | bytes 688136 | tf_op jit(solution)/shard_map/ppermute | solution.py:406
  99.6 4.4 %place.6.refs_2_ = f32[3,768,768]{2,1,0:T(8,128)S(1)} custom-call(bf16[4,224,128]{2,1,0:T(8,128)(2,1)S(1)} %collective-permute-done.11.refs_0_, bf16[4,224,128]{2,1,0:T(8,128)(2,1)S(1)} %collective-permute-done.13.refs_1_, f32[3,768,768]{2,1,0:T(8,128)S(1)} %place.5.refs_2_), custom_call_target="tpu_custom_call", output_to_operand_aliasing={{}: (2, {})} | custom-call | flops 10871635968 | bytes 7077888 | tf_op jit(solution)/shard_map/place/pallas_call | solution.py:376
  104.0 4.4 %place.7.refs_2_ = f32[3,768,768]{2,1,0:T(8,128)S(1)} custom-call(bf16[4,224,128]{2,1,0:T(8,128)(2,1)S(1)} %collective-permute-done.9.refs_0_, bf16[4,224,128]{2,1,0:T(8,128)(2,1)S(1)} %collective-permute-done.12.refs_1_, f32[3,768,768]{2,1,0:T(8,128)S(1)} %place.6.refs_2_), custom_call_target="tpu_custom_call", output_to_operand_aliasing={{}: (2, {})} | custom-call | flops 10871635968 | bytes 7077888 | tf_op jit(solution)/shard_map/place/pallas_call | solution.py:376
  108.4 4.6 %place.8.refs_1_ = f32[3,768,768]{2,1,0:T(8,128)S(1)} custom-call(bf16[4,224,128]{2,1,0:T(8,128)(2,1)S(1)} %collective-permute-done.7.refs_0_, bf16[4,224,128]{2,1,0:T(8,128)(2,1)S(1)} %collective-permute-done.10.refs_1_, f32[3,768,768]{2,1,0:T(8,128)S(1)} %place.7.refs_2_), custom_call_target="tpu_custom_call", output_to_operand_aliasing={{}: (2, {})} | custom-call | flops 10871635968 | bytes 7077888 | tf_op jit(solution)/shard_map/place/pallas_call | solution.py:376
  113.0 3.7 %place.9 = bf16[3,768,768]{2,1,0:T(8,128)(2,1)} custom-call(bf16[4,224,128]{2,1,0:T(8,128)(2,1)S(1)} %collective-permute-done.8.refs_0_, f32[3,768,768]{2,1,0:T(8,128)S(1)} %place.8.refs_1_), custom_call_target="tpu_custom_call" | custom-call | flops 5435817984 | bytes 7077888 | tf_op jit(solution)/shard_map/place/pallas_call | solution.py:376
  (54 shorter events, 12.3 us)
Async XLA Ops:
  0.6 24.0 %copy-start = (bf16[4,8,4096]{2,1,0:T(8,128)(2,1)S(1)}, bf16[4,8,4096]{2,1,0:T(8,128)(2,1)}, u32[]{:S(2)}) copy-start(bf16[4,8,4096]{2,1,0:T(8,128)(2,1)} %param.19) | copy-start | bytes 786436
  0.6 43.4 %copy-start.2 = (s32[1,192]{1,0:T(1,128)S(1)}, s32[1,192]{1,0:T(1,128)}, u32[]{:S(2)}) copy-start(s32[1,192]{1,0:T(1,128)} %param.15) | copy-start | bytes 2308
  8.9 6.1 %collective-permute-start = (bf16[16,96,128]{2,1,0:T(8,128)(2,1)}, bf16[16,96,128]{2,1,0:T(8,128)(2,1)S(1)}, u32[]{:S(2)}, u32[]{:S(2)}) collective-permute-start(bf16[16,96,128]{2,1,0:T(8,128)(2,1)} %get-tuple-element.12), channel_id=1, source_target_pairs={{0,1},{1,0},{2,3},{3,2},{4,5},{5,4},{6,7},{7,6},{8,9},{9,8},{10,11... | collective-permute-start | bytes 1179656 | tf_op jit(solution)/shard_map/ppermute | solution.py:406
  16.8 21.1 %all-to-all-start = ((bf16[16,96,128]{2,1,0:T(8,128)(2,1)}), bf16[16,96,128]{2,1,0:T(8,128)(2,1)S(1)}, u32[]{:S(2)}, u32[]{:S(2)}) async-start(bf16[16,96,128]{2,1,0:T(8,128)(2,1)} %add.17), calls=%async_computation | async-start | bytes 786432 | tf_op jit(solution)/shard_map/all_to_all | solution.py:448
  40.0 11.4 %all-to-all-start.1 = ((bf16[8,96,128]{2,1,0:T(8,128)(2,1)}), bf16[8,96,128]{2,1,0:T(8,128)(2,1)S(1)}, u32[]{:S(2)}, u32[]{:S(2)}) async-start(bf16[8,96,128]{2,1,0:T(8,128)(2,1)} %broadcast_in_dim.9), calls=%async_computation.1 | async-start | bytes 393216 | tf_op jit(solution)/shard_map/all_to_all | solution.py:452
  51.3 2.5 %copy-start.1 = (bf16[8,96,128]{2,1,0:T(8,128)(2,1)}, bf16[8,96,128]{2,1,0:T(8,128)(2,1)S(1)}, u32[]{:S(2)}) copy-start(bf16[8,96,128]{2,1,0:T(8,128)(2,1)S(1)} %all-to-all-done.1.refs_5_) | copy-start | bytes 589828
  51.3 2.5 %collective-permute-start.1 = (bf16[8,96,128]{2,1,0:T(8,128)(2,1)S(1)}, bf16[8,96,128]{2,1,0:T(8,128)(2,1)S(1)}, u32[]{:S(2)}, u32[]{:S(2)}) collective-permute-start(bf16[8,96,128]{2,1,0:T(8,128)(2,1)S(1)} %all-to-all-done.1.refs_5_), channel_id=1, source_target_pairs={{0,1},{1,0},{2,3},{3,2},{4,5},{5,4},{6,7},{7,6},{8,9},{9,8},{10,11... | collective-permute-start | bytes 589832 | tf_op jit(solution)/shard_map/ppermute | solution.py:406
  51.3 9.4 %collective-permute-start.2 = (bf16[8,96,128]{2,1,0:T(8,128)(2,1)S(1)}, bf16[8,96,128]{2,1,0:T(8,128)(2,1)S(1)}, u32[]{:S(2)}, u32[]{:S(2)}) collective-permute-start(bf16[8,96,128]{2,1,0:T(8,128)(2,1)S(1)} %all-to-all-done.1.refs_5_), channel_id=1, source_target_pairs={{0,2},{2,0},{1,3},{3,1},{4,6},{6,4},{5,7},{7,5},{8,10},{10,8},{9,1... | collective-permute-start | bytes 589832 | tf_op jit(solution)/shard_map/ppermute | solution.py:406
  51.9 10.5 %collective-permute-start.3 = (bf16[8,96,128]{2,1,0:T(8,128)(2,1)S(1)}, bf16[8,96,128]{2,1,0:T(8,128)(2,1)S(1)}, u32[]{:S(2)}, u32[]{:S(2)}) collective-permute-start(bf16[8,96,128]{2,1,0:T(8,128)(2,1)S(1)} %all-to-all-done.1.refs_5_), channel_id=1, source_target_pairs={{0,3},{1,2},{2,1},{3,0},{4,7},{5,6},{6,5},{7,4},{8,11},{9,10},{10,... | collective-permute-start | bytes 589832 | tf_op jit(solution)/shard_map/ppermute | solution.py:460
  53.9 0.7 copy-start.5
  60.8 1.6 %copy-start.3 = (bf16[8,96,128]{2,1,0:T(8,128)(2,1)}, bf16[8,96,128]{2,1,0:T(8,128)(2,1)S(1)}, u32[]{:S(2)}) copy-start(bf16[8,96,128]{2,1,0:T(8,128)(2,1)S(1)} %collective-permute-done.2.refs_5_) | copy-start | bytes 589828
  62.4 0.7 copy-start.4
  71.6 4.2 %collective-permute-start.4 = (bf16[1,224,128]{2,1,0:T(8,128)(2,1)}, bf16[1,224,128]{2,1,0:T(8,128)(2,1)S(1)}, u32[]{:S(2)}, u32[]{:S(2)}) collective-permute-start(bf16[1,224,128]{2,1,0:T(8,128)(2,1)} %get-tuple-element.17), channel_id=1, source_target_pairs={{0,1},{1,0},{2,3},{3,2},{4,5},{5,4},{6,7},{7,6},{8,9},{9,8},{10,11... | collective-permute-start | bytes 172040 | tf_op jit(solution)/shard_map/ppermute | solution.py:406
  71.9 5.0 %collective-permute-start.5 = (bf16[1,224,128]{2,1,0:T(8,128)(2,1)}, bf16[1,224,128]{2,1,0:T(8,128)(2,1)S(1)}, u32[]{:S(2)}, u32[]{:S(2)}) collective-permute-start(bf16[1,224,128]{2,1,0:T(8,128)(2,1)} %get-tuple-element.18), channel_id=1, source_target_pairs={{0,2},{2,0},{1,3},{3,1},{4,6},{6,4},{5,7},{7,5},{8,10},{10,8},{9,1... | collective-permute-start | bytes 172040 | tf_op jit(solution)/shard_map/ppermute | solution.py:406
  72.5 4.4 %collective-permute-start.6 = (bf16[1,224,128]{2,1,0:T(8,128)(2,1)}, bf16[1,224,128]{2,1,0:T(8,128)(2,1)S(1)}, u32[]{:S(2)}, u32[]{:S(2)}) collective-permute-start(bf16[1,224,128]{2,1,0:T(8,128)(2,1)} %get-tuple-element.19), channel_id=1, source_target_pairs={{0,3},{1,2},{2,1},{3,0},{4,7},{5,6},{6,5},{7,4},{8,11},{9,10},{10,... | collective-permute-start | bytes 172040 | tf_op jit(solution)/shard_map/ppermute | solution.py:514
  76.9 11.2 %collective-permute-start.11 = (bf16[4,224,128]{2,1,0:T(8,128)(2,1)S(1)}, bf16[4,224,128]{2,1,0:T(8,128)(2,1)S(1)}, u32[]{:S(2)}, u32[]{:S(2)}) collective-permute-start(bf16[4,224,128]{2,1,0:T(8,128)(2,1)S(1)} %constant_dynamic-update-slice_fusion.refs_0_), channel_id=1, source_target_pairs={{0,8},{4,12},{8,0},{12,4},{16,24},{20,28},{24,16},{28,20},{1,9},{5... | collective-permute-start | bytes 688136 | tf_op jit(solution)/shard_map/ppermute | solution.py:406
  77.1 22.5 %collective-permute-start.13 = (bf16[4,224,128]{2,1,0:T(8,128)(2,1)S(1)}, bf16[4,224,128]{2,1,0:T(8,128)(2,1)S(1)}, u32[]{:S(2)}, u32[]{:S(2)}) collective-permute-start(bf16[4,224,128]{2,1,0:T(8,128)(2,1)S(1)} %constant_dynamic-update-slice_fusion.refs_0_), channel_id=1, source_target_pairs={{0,4},{4,0},{8,12},{12,8},{16,20},{20,16},{24,28},{28,24},{1,5},{5... | collective-permute-start | bytes 688136 | tf_op jit(solution)/shard_map/ppermute | solution.py:406
  78.4 19.2 %collective-permute-start.9 = (bf16[4,224,128]{2,1,0:T(8,128)(2,1)S(1)}, bf16[4,224,128]{2,1,0:T(8,128)(2,1)S(1)}, u32[]{:S(2)}, u32[]{:S(2)}) collective-permute-start(bf16[4,224,128]{2,1,0:T(8,128)(2,1)S(1)} %constant_dynamic-update-slice_fusion.refs_0_), channel_id=1, source_target_pairs={{0,16},{4,20},{8,24},{12,28},{16,0},{20,4},{24,8},{28,12},{1,17},{... | collective-permute-start | bytes 688136 | tf_op jit(solution)/shard_map/ppermute | solution.py:406
  79.6 18.8 %collective-permute-start.7 = (bf16[4,224,128]{2,1,0:T(8,128)(2,1)S(1)}, bf16[4,224,128]{2,1,0:T(8,128)(2,1)S(1)}, u32[]{:S(2)}, u32[]{:S(2)}) collective-permute-start(bf16[4,224,128]{2,1,0:T(8,128)(2,1)S(1)} %constant_dynamic-update-slice_fusion.refs_0_), channel_id=1, source_target_pairs={{0,24},{4,28},{8,16},{12,20},{16,8},{20,12},{24,0},{28,4},{1,25},{... | collective-permute-start | bytes 688136 | tf_op jit(solution)/shard_map/ppermute | solution.py:406
  88.1 15.9 %collective-permute-start.12 = (bf16[4,224,128]{2,1,0:T(8,128)(2,1)S(1)}, bf16[4,224,128]{2,1,0:T(8,128)(2,1)S(1)}, u32[]{:S(2)}, u32[]{:S(2)}) collective-permute-start(bf16[4,224,128]{2,1,0:T(8,128)(2,1)S(1)} %collective-permute-done.11.refs_0_), channel_id=1, source_target_pairs={{0,4},{4,0},{8,12},{12,8},{16,20},{20,16},{24,28},{28,24},{1,5},{5... | collective-permute-start | bytes 688136 | tf_op jit(solution)/shard_map/ppermute | solution.py:406
  97.6 10.8 %collective-permute-start.10 = (bf16[4,224,128]{2,1,0:T(8,128)(2,1)S(1)}, bf16[4,224,128]{2,1,0:T(8,128)(2,1)S(1)}, u32[]{:S(2)}, u32[]{:S(2)}) collective-permute-start(bf16[4,224,128]{2,1,0:T(8,128)(2,1)S(1)} %collective-permute-done.9.refs_0_), channel_id=1, source_target_pairs={{0,4},{4,0},{8,12},{12,8},{16,20},{20,16},{24,28},{28,24},{1,5},{5... | collective-permute-start | bytes 688136 | tf_op jit(solution)/shard_map/ppermute | solution.py:406
  98.4 14.6 %collective-permute-start.8 = (bf16[4,224,128]{2,1,0:T(8,128)(2,1)S(1)}, bf16[4,224,128]{2,1,0:T(8,128)(2,1)S(1)}, u32[]{:S(2)}, u32[]{:S(2)}) collective-permute-start(bf16[4,224,128]{2,1,0:T(8,128)(2,1)S(1)} %collective-permute-done.7.refs_0_), channel_id=1, source_target_pairs={{0,4},{4,0},{8,12},{12,8},{16,20},{20,16},{24,28},{28,24},{1,5},{5... | collective-permute-start | bytes 688136 | tf_op jit(solution)/shard_map/ppermute | solution.py:406
where the time goes:
time: 118 us; the launch traced here: 117 us
  Pallas kernels  46.8 us (40%)
  waiting for transfers between devices  34.5 us (29%)
  starting transfers between devices  23.2 us (20%)
  local copies, waits for them, and re-layouts  7.01 us (6%)
  other arithmetic  4.16 us (4%)
    pallas_call x5, Pallas kernels, place_call(): pl.pallas_call(functools.partial(place_kernel, len(stacks), acc is not No...  19.7 us
    pallas_call x2, Pallas kernels, field_call(): pl.pallas_call(functools.partial(field_kernel, groups, size, acc is not N...  14.7 us
    ppermute x12, waiting for transfers between devices, swap(): return lax.ppermute(value, axis, [(i, i ^ mask) for i in range(size)])  13.5 us
    all_to_all x1, waiting for transfers between devices, on_device(): lax.all_to_all(held, ('batch', 'row'), split_axis=0, concat_axis=0, tiled...  13 us
    pallas_call x2, Pallas kernels, moments_call(): pl.pallas_call(functools.partial(moments_kernel, group, count, fresh), ou...  12.3 us
    ppermute x12, starting transfers between devices, swap(): return lax.ppermute(value, axis, [(i, i ^ mask) for i in range(size)])  9.5 us
    all_to_all x1, starting transfers between devices, on_device(): lax.all_to_all(held, ('batch', 'row'), split_axis=0, concat_axis=0, tiled...  7.85 us
    all_to_all x1, waiting for transfers between devices, on_device(): lax.all_to_all(jnp.broadcast_to(mine, (owners, lines, LANES)), 'batch', s...  6.35 us
  transfers between devices with their start and end apart: 16, of which 6 were waited for; matrix products, arithmetic and copies ran while one was open for 4% of the time, Pallas kernels for 24%

commit v1 on v0

--- a/solution.py
+++ b/solution.py
@@ -40,7 +40,7 @@
         centre.append(column)
     for t in range(pts_ref.shape[2] // LANES):
         here = pl.ds(t * LANES, LANES)
-        delta = [pts_ref[0, pl.ds(axis, 1), here] - centre[axis] for axis in range(3)]
+        delta = [pts_ref[axis, :, here] - centre[axis] for axis in range(3)]
         square = delta[0] * delta[0] + delta[1] * delta[1] + delta[2] * delta[2] + 0.01
         inverse = lax.rsqrt(square)
         dist_ref[t] = square * inverse
@@ -183,40 +183,42 @@
         out_specs=[VMEM] * len(out),
         scratch_shapes=table_scratch(count, points),
         cost_estimate=table_cost(count, points),
+        compiler_params=pltpu.CompilerParams(vmem_limit_bytes=20 << 20),
         name="moments",
     )(*args)
 
 
-def field_kernel(groups, size, carried, kept, last, *refs):
+def field_kernel(groups, size, carried, kept, last, tile, *refs):
     (atoms_ref, pos_ref, blocks_ref, widths_ref, pts_ref), refs = refs[:5], refs[5:]
     tabs, refs = refs[: len(groups)], refs[len(groups) :]
     count = len(groups) * size
     if carried:
         acc_in, refs = refs[0], refs[1:]
     if last:
-        (phi_ref, w_ref, marks_ref), outs, refs = refs[:3], refs[3:7], refs[7:]
+        (phi_ref, w_ref, label_ref), outs, refs = refs[:3], refs[3:7], refs[7:]
     else:
         acc_ref, refs = refs[0], refs[1:]
     if kept:
         plane_ref, refs = refs[0], refs[1:]
-        for order, tab in enumerate(tabs):
-            plane_ref[order ^ lax.axis_index("col")] = tab[lax.axis_index("batch")]
     dist_ref, polar_ref, side_ref, scale_ref = refs[:4]
     if last:
-        acc_ref, oper_ref = refs[4:]
+        acc_ref, oper_ref, marks_ref = refs[4:7]
     points = pts_ref.shape[2]
     finders = [atom_finder(group, atoms_ref) for group in groups]
     prepare([atom_at(i) for atom_at in finders for i in range(size)], pos_ref, pts_ref, dist_ref, polar_ref, side_ref)
     prepare_shells(widths_ref, scale_ref)
     acc_ref[...] = acc_in[...] if carried else jnp.zeros_like(acc_ref)
-
-    def body(i, carry, tab_ref, atom_at, base):
-        k = base + i
+    if kept:
+        for order in range(len(groups)):
+            plane_ref[order ^ lax.axis_index("col")] = tabs[order][lax.axis_index("batch")]
+
+    def body(i, carry, order, atom_at):
+        k = order * size + i
         blocks = blocks_ref[atom_at(i)]
 
         live, half = S, S // 2
         middle, scale = shell_columns(blocks, live, scale_ref)
-        table = tab_ref[i].astype(jnp.float32)
+        table = tabs[order][i].astype(jnp.float32)
         lines = []
         for c in range(3):
             block = table[c * (S // 2) : c * (S // 2) + half]
@@ -241,11 +243,16 @@
         return carry
 
     for order, atom_at in enumerate(finders):
-        step = functools.partial(body, tab_ref=tabs[order], atom_at=atom_at, base=order * size)
+        step = functools.partial(body, order=order, atom_at=atom_at)
         lax.fori_loop(0, size, step, 0, unroll=4)
     if last:
         piece = phi_ref.shape[1] // 2
         third = piece // 3
+        for h in range(2):
+            strips = [label_ref[:, h * piece + b * third : h * piece + (b + 1) * third] for b in range(3)]
+            inner = jnp.concatenate(strips, axis=0) - h * tile
+            digits = [(inner >> 5).astype(jnp.float32), (inner & 31).astype(jnp.float32)]
+            marks_ref[h] = jnp.concatenate(digits + [jnp.zeros((2, third), jnp.float32)], axis=0)
         sides = (lax.axis_index("row"), lax.axis_index("col"))
         halves = [[flip ^ side for flip in range(2)] for side in sides]
         spans = [[pl.ds(pl.multiple_of(h * piece, 32), piece) for h in pair] for pair in halves]
@@ -288,18 +295,23 @@
         args += ends
         third = ends[0].shape[1] // 6
         out = [jax.ShapeDtypeStruct((1, 7 * third, LANES), jnp.bfloat16)] * 4
-        scratch += [pltpu.VMEM((24, points), jnp.float32), pltpu.VMEM(ends[0].shape[1:], jnp.bfloat16)]
+        scratch += [
+            pltpu.VMEM((24, points), jnp.float32),
+            pltpu.VMEM(ends[0].shape[1:], jnp.bfloat16),
+            pltpu.VMEM((2, 8, third), jnp.float32),
+        ]
     else:
         out = [jax.ShapeDtypeStruct((24, points), jnp.float32)]
     if keep:
         out.append(jax.ShapeDtypeStruct((len(groups),) + tables[0].shape[1:], jnp.bfloat16))
     return pl.pallas_call(
-        functools.partial(field_kernel, groups, size, acc is not None, keep, last),
+        functools.partial(field_kernel, groups, size, acc is not None, keep, last, NB // 2),
         out_shape=out,
         in_specs=[SMEM] * 4 + [VMEM] * (len(args) - 4),
         out_specs=[VMEM] * len(out),
         scratch_shapes=scratch,
         cost_estimate=table_cost(count, points),
+        compiler_params=pltpu.CompilerParams(vmem_limit_bytes=20 << 20),
         name="field",
     )(*args)
 
@@ -435,7 +447,7 @@
     plane = ("row", "col")
     across = [(i, i ^ 3) for i in range(parts * sides)]
     half, group = count // 2, count // 4
-    shared = (atoms, atom_positions, shell_blocks, shell_widths, points)
+    shared = (atoms, atom_positions, shell_blocks, shell_widths, jnp.swapaxes(points, 0, 1))
     wanted = ((sides, None, 0), (sides, None, 1)) if dense else (0, half)
     listed = [(holding, f & 1, f >> 1) if dense else f * group for f in range(4)]
     other, weighted = moments_call(
@@ -499,10 +511,7 @@
         tables = [table[place * group : (place + 1) * group] for place in range(4)]
     piece = labels.shape[0] // parts
     tile = NB // parts
-    inner = labels.reshape(parts, 3, piece // 3) - jnp.arange(parts)[:, None, None] * tile
-    marks = jnp.concatenate([inner // 32, inner % 32, inner[:, :2] * 0], axis=1)
-    marks = marks.astype(jnp.float32)
-    ends = [basis_values, weights, marks]
+    ends = [basis_values, weights, basis_index]
     spread = functools.partial(field_call, size=group, shared=shared, keep=dense)
     field, *ours = spread((listed[0], listed[2]), tables=[tables[0], tables[2]])
     load = spread((listed[1], listed[3]), tables=[tables[1], tables[3]], acc=field, ends=ends)

time: 118 us -> 116 us (0.983)
  blocking collectives: 0 us -> 11.1 us
  Pallas kernels: 46.8 us -> 41.7 us
  starting transfers between devices: 23.2 us -> 19.8 us
  other arithmetic: 4.16 us -> 0.96 us
  waiting for transfers between devices: 34.5 us -> 32 us
  local copies, waits for them, and re-layouts: 7.01 us -> 8.31 us
    all_to_all x0 -> x1, blocking collectives: none -> 11.1 us  [on_device(): lax.all_to_all(jnp.broadcast_to(mine, (owners, lines, LANES)), 'batch', s...]
    all_to_all x1 -> x0, waiting for transfers between devices: 6.35 us -> none  [on_device(): lax.all_to_all(jnp.broadcast_to(mine, (owners, lines, LANES)), 'batch', s...]
    all_to_all x1 -> x0, starting transfers between devices: 3.58 us -> none  [on_device(): lax.all_to_all(jnp.broadcast_to(mine, (owners, lines, LANES)), 'batch', s...]
    pallas_call x2, Pallas kernels: 14.7 us -> 12.1 us  [field_call(): pl.pallas_call(functools.partial(field_kernel, groups, size, acc is not N...]
    pallas_call x2, Pallas kernels: 12.3 us -> 10 us  [moments_call(): pl.pallas_call(functools.partial(moments_kernel, group, count, fresh), ou...]
    ppermute x12, waiting for transfers between devices: 13.5 us -> 15.7 us  [swap(): return lax.ppermute(value, axis, [(i, i ^ mask) for i in range(size)])]
    unnamed x18 -> x38, local copies, waits for them, and re-layouts: 4.82 us -> 6.97 us
    ppermute x1, waiting for transfers between devices: 1.62 us -> 3.29 us  [on_device(): beyond = lax.ppermute(own, plane, across)]
  transfers between devices with their start and end apart: 16 -> 15, of which waited for: 6 -> 6; matrix products, arithmetic and copies ran while one was open for 4% -> 1% of each run, Pallas kernels for 24% -> 22%
where the time goes in v1:
time: 116 us; the launch traced here: 115 us
  Pallas kernels  41.7 us (36%)
  waiting for transfers between devices  32 us (28%)
  starting transfers between devices  19.8 us (17%)
  blocking collectives  11.1 us (10%)
  local copies, waits for them, and re-layouts  8.31 us (7%)
    pallas_call x5, Pallas kernels, place_call(): pl.pallas_call(functools.partial(place_kernel, len(stacks), acc is not No...  19.7 us
    ppermute x12, waiting for transfers between devices, swap(): return lax.ppermute(value, axis, [(i, i ^ mask) for i in range(size)])  15.7 us
    all_to_all x1, waiting for transfers between devices, on_device(): lax.all_to_all(held, ('batch', 'row'), split_axis=0, concat_axis=0, tiled...  13 us
    pallas_call x2, Pallas kernels, field_call(): pl.pallas_call(functools.partial(field_kernel, groups, size, acc is not N...  12.1 us
    all_to_all x1, blocking collectives, on_device(): lax.all_to_all(jnp.broadcast_to(mine, (owners, lines, LANES)), 'batch', s...  11.1 us
    pallas_call x2, Pallas kernels, moments_call(): pl.pallas_call(functools.partial(moments_kernel, group, count, fresh), ou...  10 us
    ppermute x12, starting transfers between devices, swap(): return lax.ppermute(value, axis, [(i, i ^ mask) for i in range(size)])  9.65 us
    all_to_all x1, starting transfers between devices, on_device(): lax.all_to_all(held, ('batch', 'row'), split_axis=0, concat_axis=0, tiled...  7.86 us
  transfers between devices with their start and end apart: 15, of which 6 were waited for; matrix products, arithmetic and copies ran while one was open for 1% of the time, Pallas kernels for 22%

profile of v1, /device:TPU:0, one launch (start us, length us, event | category | flops | bytes accessed | tf_op | source)
XLA Modules:
  0.0 115.3 jit_solution(8217340127717879743)
XLA Ops:
  0.7 1.2 %copy-done.1 = bf16[1,192,2048]{2,1,0:T(8,128)(2,1)S(1)} copy-done((bf16[1,192,2048]{2,1,0:T(8,128)(2,1)S(1)}, bf16[1,192,2048]{2,1,0:T(8,128)(2,1)}, u32[]{:S(2)}) %copy-start.1) | copy-done | bytes 786456
  1.9 1.0 copy-done.3
  6.9 5.4 %moments.2 = (bf16[16,96,128]{2,1,0:T(8,128)(2,1)S(1)}, f32[3,2048]{1,0:T(4,128)S(1)}) custom-call(s32[32]{0:T(128)S(1)} %bitcast.20, f32[3,32]{1,0:T(4,128)S(1)} %copy-done.8, s32[32]{0:T(128)S(1)} %copy-done.13, f32[64]{0:T(128)S(1)} %copy-done.15, f32[3,1,2048]{2,1,0:T(1,128)S(1)} %bitcast.16, bf16[1,192,2048]{2,1,0:T(8,128)(2,1)S(1)} %copy-done.1, ...), custom_call_target="tpu_custom_call" | custom-call | flops 805306368 | bytes 2097152 | tf_op jit(solution)/shard_map/moments/pallas_call | solution.py:179
  12.9 4.6 %moments.3 = bf16[16,96,128]{2,1,0:T(8,128)(2,1)S(1)} custom-call(s32[32]{0:T(128)S(1)} %bitcast.21, f32[3,32]{1,0:T(4,128)S(1)} %copy-done.8, s32[32]{0:T(128)S(1)} %copy-done.13, f32[64]{0:T(128)S(1)} %copy-done.15, f32[3,1,2048]{2,1,0:T(1,128)S(1)} %bitcast.17, f32[3,2048]{1,0:T(4,128)S(1)} %get-tuple-element.11.refs_5_), custom_call_target="tpu_custom_call" | custom-call | flops 805306368 | bytes 2097152 | tf_op jit(solution)/shard_map/moments/pallas_call | solution.py:179
  18.4 7.9 %all-to-all-start = ((bf16[16,96,128]{2,1,0:T(8,128)(2,1)}), bf16[16,96,128]{2,1,0:T(8,128)(2,1)S(1)}, u32[]{:S(2)}, u32[]{:S(2)}) async-start(bf16[16,96,128]{2,1,0:T(8,128)(2,1)} %add.10), calls=%async_computation | async-start | bytes 786432 | tf_op jit(solution)/shard_map/all_to_all | solution.py:460
  26.5 13.0 %all-to-all-done = bf16[16,96,128]{2,1,0:T(8,128)(2,1)S(1)} async-done(((bf16[16,96,128]{2,1,0:T(8,128)(2,1)}), bf16[16,96,128]{2,1,0:T(8,128)(2,1)S(1)}, u32[]{:S(2)}, u32[]{:S(2)}) %all-to-all-start) | async-done | bytes 393248 | tf_op jit(solution)/shard_map/all_to_all | solution.py:460
  41.0 11.1 %all_to_all.10.refs_5_ = bf16[8,96,128]{2,1,0:T(8,128)(2,1)S(1)} all-to-all(bf16[8,96,128]{2,1,0:T(8,128)(2,1)S(1)} %broadcast_in_dim.8), channel_id=1, replica_groups=mesh['batch'=8,'row'=2,'col'=2] {'batch'}, dimensions={0} | all-to-all | bytes 393216 | tf_op jit(solution)/shard_map/all_to_all | solution.py:464
  52.7 1.3 %collective-permute-start.3 = (bf16[8,96,128]{2,1,0:T(8,128)(2,1)S(1)}, bf16[8,96,128]{2,1,0:T(8,128)(2,1)S(1)}, u32[]{:S(2)}, u32[]{:S(2)}) collective-permute-start(bf16[8,96,128]{2,1,0:T(8,128)(2,1)S(1)} %all_to_all.10.refs_5_), channel_id=1, source_target_pairs={{0,3},{1,2},{2,1},{3,0},{4,7},{5,6},{6,5},{7,4},{8,11},{9,10},{10,... | collective-permute-start | bytes 589832 | tf_op jit(solution)/shard_map/ppermute | solution.py:472
  54.0 5.1 %field.2 = (f32[24,2048]{1,0:T(8,128)S(1)}, bf16[2,96,128]{2,1,0:T(8,128)(2,1)S(1)}) custom-call(s32[32]{0:T(128)S(1)} %bitcast.22, f32[3,32]{1,0:T(4,128)S(1)} %copy-done.9, s32[32]{0:T(128)S(1)} %copy-done.14, f32[64]{0:T(128)S(1)} %copy-done.16, f32[3,1,2048]{2,1,0:T(1,128)S(1)} %bitcast.18, bf16[8,96,128]{2,1,0:T(8,128)(2,1)S(1)} %all_to_all.10.refs_5_, ...), custom_call_target="tpu_custom_call" | custom-call | flops 805306368 | bytes 2097152 | tf_op jit(solution)/shard_map/field/pallas_call | solution.py:307
  59.9 3.3 %collective-permute-done.3.refs_6_ = bf16[8,96,128]{2,1,0:T(8,128)(2,1)S(1)} collective-permute-done((bf16[8,96,128]{2,1,0:T(8,128)(2,1)S(1)}, bf16[8,96,128]{2,1,0:T(8,128)(2,1)S(1)}, u32[]{:S(2)}, u32[]{:S(2)}) %collective-permute-start.3) | collective-permute-done | bytes 196640 | tf_op jit(solution)/shard_map/ppermute | solution.py:472
  63.2 7.0 %field.3 = (bf16[1,224,128]{2,1,0:T(8,128)(2,1)S(1)}, bf16[1,224,128]{2,1,0:T(8,128)(2,1)S(1)}, bf16[1,224,128]{2,1,0:T(8,128)(2,1)S(1)}, bf16[1,224,128]{2,1,0:T(8,128)(2,1)S(1)}, bf16[2,96,128]{2,1,0:T(8,128)(2,1)S(1)}) custom-call(s32[32]{0:T(128)S(1)} %bitcast.23, f32[3,32]{1,0:T(4,128)S(1)} %copy-done.9, s32[32]{0:T(128)S(1)} %copy-done.14, ...), custom_call_target="tpu_custom_call" | custom-call | flops 805306368 | bytes 2097152 | tf_op jit(solution)/shard_map/field/pallas_call | solution.py:307
  71.1 1.0 collective-permute-start.6
  72.8 2.5 %collective-permute-done.5 = bf16[1,224,128]{2,1,0:T(8,128)(2,1)S(1)} collective-permute-done((bf16[1,224,128]{2,1,0:T(8,128)(2,1)S(1)}, bf16[1,224,128]{2,1,0:T(8,128)(2,1)S(1)}, u32[]{:S(2)}, u32[]{:S(2)}) %collective-permute-start.5) | collective-permute-done | bytes 57376 | tf_op jit(solution)/shard_map/ppermute | solution.py:418
  75.6 1.2 %collective-permute-start.13 = (bf16[4,224,128]{2,1,0:T(8,128)(2,1)S(1)}, bf16[4,224,128]{2,1,0:T(8,128)(2,1)S(1)}, u32[]{:S(2)}, u32[]{:S(2)}) collective-permute-start(bf16[4,224,128]{2,1,0:T(8,128)(2,1)S(1)} %constant_dynamic-update-slice_fusion.refs_0_), channel_id=1, source_target_pairs={{0,4},{4,0},{8,12},{12,8},{16,20},{20,16},{24,28},{28,24},{1,5},{5... | collective-permute-start | bytes 688136 | tf_op jit(solution)/shard_map/ppermute | solution.py:418
  76.8 1.2 %collective-permute-start.9 = (bf16[4,224,128]{2,1,0:T(8,128)(2,1)S(1)}, bf16[4,224,128]{2,1,0:T(8,128)(2,1)S(1)}, u32[]{:S(2)}, u32[]{:S(2)}) collective-permute-start(bf16[4,224,128]{2,1,0:T(8,128)(2,1)S(1)} %constant_dynamic-update-slice_fusion.refs_0_), channel_id=1, source_target_pairs={{0,16},{4,20},{8,24},{12,28},{16,0},{20,4},{24,8},{28,12},{1,17},{... | collective-permute-start | bytes 688136 | tf_op jit(solution)/shard_map/ppermute | solution.py:418
  78.0 2.7 %collective-permute-start.7 = (bf16[4,224,128]{2,1,0:T(8,128)(2,1)S(1)}, bf16[4,224,128]{2,1,0:T(8,128)(2,1)S(1)}, u32[]{:S(2)}, u32[]{:S(2)}) collective-permute-start(bf16[4,224,128]{2,1,0:T(8,128)(2,1)S(1)} %constant_dynamic-update-slice_fusion.refs_0_), channel_id=1, source_target_pairs={{0,24},{4,28},{8,16},{12,20},{16,8},{20,12},{24,0},{28,4},{1,25},{... | collective-permute-start | bytes 688136 | tf_op jit(solution)/shard_map/ppermute | solution.py:418
  80.7 2.6 %place.5.refs_2_ = f32[3,768,768]{2,1,0:T(8,128)S(1)} custom-call(bf16[4,224,128]{2,1,0:T(8,128)(2,1)S(1)} %constant_dynamic-update-slice_fusion.refs_0_), custom_call_target="tpu_custom_call" | custom-call | flops 5435817984 | bytes 7077888 | tf_op jit(solution)/shard_map/place/pallas_call | solution.py:388
  83.3 3.1 %collective-permute-done.11.refs_0_ = bf16[4,224,128]{2,1,0:T(8,128)(2,1)S(1)} collective-permute-done((bf16[4,224,128]{2,1,0:T(8,128)(2,1)S(1)}, bf16[4,224,128]{2,1,0:T(8,128)(2,1)S(1)}, u32[]{:S(2)}, u32[]{:S(2)}) %collective-permute-start.11) | collective-permute-done | bytes 229408 | tf_op jit(solution)/shard_map/ppermute | solution.py:418
  86.7 9.3 %collective-permute-done.9.refs_0_ = bf16[4,224,128]{2,1,0:T(8,128)(2,1)S(1)} collective-permute-done((bf16[4,224,128]{2,1,0:T(8,128)(2,1)S(1)}, bf16[4,224,128]{2,1,0:T(8,128)(2,1)S(1)}, u32[]{:S(2)}, u32[]{:S(2)}) %collective-permute-start.9) | collective-permute-done | bytes 229408 | tf_op jit(solution)/shard_map/ppermute | solution.py:418
  96.8 1.2 %collective-permute-start.8 = (bf16[4,224,128]{2,1,0:T(8,128)(2,1)S(1)}, bf16[4,224,128]{2,1,0:T(8,128)(2,1)S(1)}, u32[]{:S(2)}, u32[]{:S(2)}) collective-permute-start(bf16[4,224,128]{2,1,0:T(8,128)(2,1)S(1)} %collective-permute-done.7.refs_0_), channel_id=1, source_target_pairs={{0,4},{4,0},{8,12},{12,8},{16,20},{20,16},{24,28},{28,24},{1,5},{5... | collective-permute-start | bytes 688136 | tf_op jit(solution)/shard_map/ppermute | solution.py:418
  98.0 4.4 %place.6.refs_2_ = f32[3,768,768]{2,1,0:T(8,128)S(1)} custom-call(bf16[4,224,128]{2,1,0:T(8,128)(2,1)S(1)} %collective-permute-done.11.refs_0_, bf16[4,224,128]{2,1,0:T(8,128)(2,1)S(1)} %collective-permute-done.13.refs_1_, f32[3,768,768]{2,1,0:T(8,128)S(1)} %place.5.refs_2_), custom_call_target="tpu_custom_call", output_to_operand_aliasing={{}: (2, {})} | custom-call | flops 10871635968 | bytes 7077888 | tf_op jit(solution)/shard_map/place/pallas_call | solution.py:388
  102.4 4.4 %place.7.refs_2_ = f32[3,768,768]{2,1,0:T(8,128)S(1)} custom-call(bf16[4,224,128]{2,1,0:T(8,128)(2,1)S(1)} %collective-permute-done.9.refs_0_, bf16[4,224,128]{2,1,0:T(8,128)(2,1)S(1)} %collective-permute-done.12.refs_1_, f32[3,768,768]{2,1,0:T(8,128)S(1)} %place.6.refs_2_), custom_call_target="tpu_custom_call", output_to_operand_aliasing={{}: (2, {})} | custom-call | flops 10871635968 | bytes 7077888 | tf_op jit(solution)/shard_map/place/pallas_call | solution.py:388
  106.8 4.6 %place.8.refs_1_ = f32[3,768,768]{2,1,0:T(8,128)S(1)} custom-call(bf16[4,224,128]{2,1,0:T(8,128)(2,1)S(1)} %collective-permute-done.7.refs_0_, bf16[4,224,128]{2,1,0:T(8,128)(2,1)S(1)} %collective-permute-done.10.refs_1_, f32[3,768,768]{2,1,0:T(8,128)S(1)} %place.7.refs_2_), custom_call_target="tpu_custom_call", output_to_operand_aliasing={{}: (2, {})} | custom-call | flops 10871635968 | bytes 7077888 | tf_op jit(solution)/shard_map/place/pallas_call | solution.py:388
  111.4 3.7 %place.9 = bf16[3,768,768]{2,1,0:T(8,128)(2,1)} custom-call(bf16[4,224,128]{2,1,0:T(8,128)(2,1)S(1)} %collective-permute-done.8.refs_0_, f32[3,768,768]{2,1,0:T(8,128)S(1)} %place.8.refs_1_), custom_call_target="tpu_custom_call" | custom-call | flops 5435817984 | bytes 7077888 | tf_op jit(solution)/shard_map/place/pallas_call | solution.py:388
  (66 shorter events, 11.5 us)
Async XLA Ops:
  0.6 25.7 %copy-start = (bf16[4,8,4096]{2,1,0:T(8,128)(2,1)S(1)}, bf16[4,8,4096]{2,1,0:T(8,128)(2,1)}, u32[]{:S(2)}) copy-start(bf16[4,8,4096]{2,1,0:T(8,128)(2,1)} %param.19) | copy-start | bytes 786436
  0.6 53.3 %copy-start.12 = (s32[1,32]{1,0:T(1,128)S(1)}, s32[1,32]{1,0:T(1,128)}, u32[]{:S(2)}) copy-start(s32[1,32]{1,0:T(1,128)} %param.14) | copy-start | bytes 388
  0.7 53.3 %copy-start.9 = (f32[3,32]{1,0:T(4,128)S(1)}, f32[3,32]{1,0:T(4,128)}, u32[]{:S(2)}) copy-start(f32[3,32]{1,0:T(4,128)} %refs_1_.7) | copy-start | bytes 1156
  0.7 53.3 %copy-start.14 = (s32[32]{0:T(128)S(1)}, s32[32]{0:T(128)}, u32[]{:S(2)}) copy-start(s32[32]{0:T(128)} %refs_2_.7) | copy-start | bytes 388
  0.7 53.3 %copy-start.16 = (f32[64]{0:T(128)S(1)}, f32[64]{0:T(128)}, u32[]{:S(2)}) copy-start(f32[64]{0:T(128)} %refs_3_.7) | copy-start | bytes 772
  6.9 47.1 %copy-start.5 = (f32[1,3,2048]{2,0,1:T(1,128)S(1)}, f32[1,3,2048]{2,0,1:T(1,128)}, u32[]{:S(2)}) copy-start(f32[1,3,2048]{2,0,1:T(1,128)} %param.12) | copy-start | bytes 73732
  12.3 50.8 %copy-start.2 = (bf16[1,192,2048]{2,1,0:T(8,128)(2,1)S(1)}, bf16[1,192,2048]{2,1,0:T(8,128)(2,1)}, u32[]{:S(2)}) copy-start(bf16[1,192,2048]{2,1,0:T(8,128)(2,1)} %refs_8_.1) | copy-start | bytes 2359300
  12.4 50.8 %copy-start.7 = (f32[1,2048]{1,0:T(1,128)S(1)}, f32[1,2048]{1,0:T(1,128)}, u32[]{:S(2)}) copy-start(f32[1,2048]{1,0:T(1,128)} %refs_9_.1) | copy-start | bytes 24580
  12.4 50.8 %copy-start.10 = (s32[1,192]{1,0:T(1,128)S(1)}, s32[1,192]{1,0:T(1,128)}, u32[]{:S(2)}) copy-start(s32[1,192]{1,0:T(1,128)} %refs_10_.1) | copy-start | bytes 2308
  12.4 5.1 %collective-permute-start = (bf16[16,96,128]{2,1,0:T(8,128)(2,1)S(1)}, bf16[16,96,128]{2,1,0:T(8,128)(2,1)S(1)}, u32[]{:S(2)}, u32[]{:S(2)}) collective-permute-start(bf16[16,96,128]{2,1,0:T(8,128)(2,1)S(1)} %get-tuple-element.12), channel_id=1, source_target_pairs={{0,1},{1,0},{2,3},{3,2},{4,5},{5,4},{6,7},{7,6},{8,9},{9,8},{10,11... | collective-permute-start | bytes 1179656 | tf_op jit(solution)/shard_map/ppermute | solution.py:418
  18.4 21.1 %all-to-all-start = ((bf16[16,96,128]{2,1,0:T(8,128)(2,1)}), bf16[16,96,128]{2,1,0:T(8,128)(2,1)S(1)}, u32[]{:S(2)}, u32[]{:S(2)}) async-start(bf16[16,96,128]{2,1,0:T(8,128)(2,1)} %add.10), calls=%async_computation | async-start | bytes 786432 | tf_op jit(solution)/shard_map/all_to_all | solution.py:460
  52.1 1.9 %collective-permute-start.1 = (bf16[8,96,128]{2,1,0:T(8,128)(2,1)S(1)}, bf16[8,96,128]{2,1,0:T(8,128)(2,1)S(1)}, u32[]{:S(2)}, u32[]{:S(2)}) collective-permute-start(bf16[8,96,128]{2,1,0:T(8,128)(2,1)S(1)} %all_to_all.10.refs_5_), channel_id=1, source_target_pairs={{0,1},{1,0},{2,3},{3,2},{4,5},{5,4},{6,7},{7,6},{8,9},{9,8},{10,11... | collective-permute-start | bytes 589832 | tf_op jit(solution)/shard_map/ppermute | solution.py:418
  52.1 7.8 %collective-permute-start.2 = (bf16[8,96,128]{2,1,0:T(8,128)(2,1)S(1)}, bf16[8,96,128]{2,1,0:T(8,128)(2,1)S(1)}, u32[]{:S(2)}, u32[]{:S(2)}) collective-permute-start(bf16[8,96,128]{2,1,0:T(8,128)(2,1)S(1)} %all_to_all.10.refs_5_), channel_id=1, source_target_pairs={{0,2},{2,0},{1,3},{3,1},{4,6},{6,4},{5,7},{7,5},{8,10},{10,8},{9,1... | collective-permute-start | bytes 589832 | tf_op jit(solution)/shard_map/ppermute | solution.py:418
  52.7 10.5 %collective-permute-start.3 = (bf16[8,96,128]{2,1,0:T(8,128)(2,1)S(1)}, bf16[8,96,128]{2,1,0:T(8,128)(2,1)S(1)}, u32[]{:S(2)}, u32[]{:S(2)}) collective-permute-start(bf16[8,96,128]{2,1,0:T(8,128)(2,1)S(1)} %all_to_all.10.refs_5_), channel_id=1, source_target_pairs={{0,3},{1,2},{2,1},{3,0},{4,7},{5,6},{6,5},{7,4},{8,11},{9,10},{10,... | collective-permute-start | bytes 589832 | tf_op jit(solution)/shard_map/ppermute | solution.py:472
  70.2 2.7 %collective-permute-start.4 = (bf16[1,224,128]{2,1,0:T(8,128)(2,1)S(1)}, bf16[1,224,128]{2,1,0:T(8,128)(2,1)S(1)}, u32[]{:S(2)}, u32[]{:S(2)}) collective-permute-start(bf16[1,224,128]{2,1,0:T(8,128)(2,1)S(1)} %get-tuple-element.17), channel_id=1, source_target_pairs={{0,1},{1,0},{2,3},{3,2},{4,5},{5,4},{6,7},{7,6},{8,9},{9,8},{10,11... | collective-permute-start | bytes 172040 | tf_op jit(solution)/shard_map/ppermute | solution.py:418
  70.5 4.8 %collective-permute-start.5 = (bf16[1,224,128]{2,1,0:T(8,128)(2,1)S(1)}, bf16[1,224,128]{2,1,0:T(8,128)(2,1)S(1)}, u32[]{:S(2)}, u32[]{:S(2)}) collective-permute-start(bf16[1,224,128]{2,1,0:T(8,128)(2,1)S(1)} %get-tuple-element.18), channel_id=1, source_target_pairs={{0,2},{2,0},{1,3},{3,1},{4,6},{6,4},{5,7},{7,5},{8,10},{10,8},{9,1... | collective-permute-start | bytes 172040 | tf_op jit(solution)/shard_map/ppermute | solution.py:418
  71.1 4.2 %collective-permute-start.6 = (bf16[1,224,128]{2,1,0:T(8,128)(2,1)S(1)}, bf16[1,224,128]{2,1,0:T(8,128)(2,1)S(1)}, u32[]{:S(2)}, u32[]{:S(2)}) collective-permute-start(bf16[1,224,128]{2,1,0:T(8,128)(2,1)S(1)} %get-tuple-element.19), channel_id=1, source_target_pairs={{0,3},{1,2},{2,1},{3,0},{4,7},{5,6},{6,5},{7,4},{8,11},{9,10},{10,... | collective-permute-start | bytes 172040 | tf_op jit(solution)/shard_map/ppermute | solution.py:523
  75.3 11.1 %collective-permute-start.11 = (bf16[4,224,128]{2,1,0:T(8,128)(2,1)S(1)}, bf16[4,224,128]{2,1,0:T(8,128)(2,1)S(1)}, u32[]{:S(2)}, u32[]{:S(2)}) collective-permute-start(bf16[4,224,128]{2,1,0:T(8,128)(2,1)S(1)} %constant_dynamic-update-slice_fusion.refs_0_), channel_id=1, source_target_pairs={{0,8},{4,12},{8,0},{12,4},{16,24},{20,28},{24,16},{28,20},{1,9},{5... | collective-permute-start | bytes 688136 | tf_op jit(solution)/shard_map/ppermute | solution.py:418
  75.6 22.5 %collective-permute-start.13 = (bf16[4,224,128]{2,1,0:T(8,128)(2,1)S(1)}, bf16[4,224,128]{2,1,0:T(8,128)(2,1)S(1)}, u32[]{:S(2)}, u32[]{:S(2)}) collective-permute-start(bf16[4,224,128]{2,1,0:T(8,128)(2,1)S(1)} %constant_dynamic-update-slice_fusion.refs_0_), channel_id=1, source_target_pairs={{0,4},{4,0},{8,12},{12,8},{16,20},{20,16},{24,28},{28,24},{1,5},{5... | collective-permute-start | bytes 688136 | tf_op jit(solution)/shard_map/ppermute | solution.py:418
  76.8 19.2 %collective-permute-start.9 = (bf16[4,224,128]{2,1,0:T(8,128)(2,1)S(1)}, bf16[4,224,128]{2,1,0:T(8,128)(2,1)S(1)}, u32[]{:S(2)}, u32[]{:S(2)}) collective-permute-start(bf16[4,224,128]{2,1,0:T(8,128)(2,1)S(1)} %constant_dynamic-update-slice_fusion.refs_0_), channel_id=1, source_target_pairs={{0,16},{4,20},{8,24},{12,28},{16,0},{20,4},{24,8},{28,12},{1,17},{... | collective-permute-start | bytes 688136 | tf_op jit(solution)/shard_map/ppermute | solution.py:418
  78.0 18.9 %collective-permute-start.7 = (bf16[4,224,128]{2,1,0:T(8,128)(2,1)S(1)}, bf16[4,224,128]{2,1,0:T(8,128)(2,1)S(1)}, u32[]{:S(2)}, u32[]{:S(2)}) collective-permute-start(bf16[4,224,128]{2,1,0:T(8,128)(2,1)S(1)} %constant_dynamic-update-slice_fusion.refs_0_), channel_id=1, source_target_pairs={{0,24},{4,28},{8,16},{12,20},{16,8},{20,12},{24,0},{28,4},{1,25},{... | collective-permute-start | bytes 688136 | tf_op jit(solution)/shard_map/ppermute | solution.py:418
  86.5 15.9 %collective-permute-start.12 = (bf16[4,224,128]{2,1,0:T(8,128)(2,1)S(1)}, bf16[4,224,128]{2,1,0:T(8,128)(2,1)S(1)}, u32[]{:S(2)}, u32[]{:S(2)}) collective-permute-start(bf16[4,224,128]{2,1,0:T(8,128)(2,1)S(1)} %collective-permute-done.11.refs_0_), channel_id=1, source_target_pairs={{0,4},{4,0},{8,12},{12,8},{16,20},{20,16},{24,28},{28,24},{1,5},{5... | collective-permute-start | bytes 688136 | tf_op jit(solution)/shard_map/ppermute | solution.py:418
  96.0 10.8 %collective-permute-start.10 = (bf16[4,224,128]{2,1,0:T(8,128)(2,1)S(1)}, bf16[4,224,128]{2,1,0:T(8,128)(2,1)S(1)}, u32[]{:S(2)}, u32[]{:S(2)}) collective-permute-start(bf16[4,224,128]{2,1,0:T(8,128)(2,1)S(1)} %collective-permute-done.9.refs_0_), channel_id=1, source_target_pairs={{0,4},{4,0},{8,12},{12,8},{16,20},{20,16},{24,28},{28,24},{1,5},{5... | collective-permute-start | bytes 688136 | tf_op jit(solution)/shard_map/ppermute | solution.py:418
  96.8 14.6 %collective-permute-start.8 = (bf16[4,224,128]{2,1,0:T(8,128)(2,1)S(1)}, bf16[4,224,128]{2,1,0:T(8,128)(2,1)S(1)}, u32[]{:S(2)}, u32[]{:S(2)}) collective-permute-start(bf16[4,224,128]{2,1,0:T(8,128)(2,1)S(1)} %collective-permute-done.7.refs_0_), channel_id=1, source_target_pairs={{0,4},{4,0},{8,12},{12,8},{16,20},{20,16},{24,28},{28,24},{1,5},{5... | collective-permute-start | bytes 688136 | tf_op jit(solution)/shard_map/ppermute | solution.py:418
  (8 other events, 6.2 us)

commit v2 on v1

--- a/solution.py
+++ b/solution.py
@@ -183,7 +183,6 @@
         out_specs=[VMEM] * len(out),
         scratch_shapes=table_scratch(count, points),
         cost_estimate=table_cost(count, points),
-        compiler_params=pltpu.CompilerParams(vmem_limit_bytes=20 << 20),
         name="moments",
     )(*args)
 
@@ -210,7 +209,8 @@
     acc_ref[...] = acc_in[...] if carried else jnp.zeros_like(acc_ref)
     if kept:
         for order in range(len(groups)):
-            plane_ref[order ^ lax.axis_index("col")] = tabs[order][lax.axis_index("batch")]
+            at = order ^ lax.axis_index("col") if len(groups) == 2 else order
+            plane_ref[at] = tabs[order][lax.axis_index("batch")]
 
     def body(i, carry, order, atom_at):
         k = order * size + i
@@ -446,18 +446,26 @@
     dense = count == every_atom and holding == parts * sides
     plane = ("row", "col")
     across = [(i, i ^ 3) for i in range(parts * sides)]
-    half, group = count // 2, count // 4
+    group = count // 4
     shared = (atoms, atom_positions, shell_blocks, shell_widths, jnp.swapaxes(points, 0, 1))
-    wanted = ((sides, None, 0), (sides, None, 1)) if dense else (0, half)
     listed = [(holding, f & 1, f >> 1) if dense else f * group for f in range(4)]
-    other, weighted = moments_call(
-        wanted[1], half, shared, phi=basis_values, dens=density_matrix, w=weights
+    third, weighted = moments_call(
+        listed[3], group, shared, phi=basis_values, dens=density_matrix, w=weights
     )
-    mate = swap(other, "col") if dense else other
-    first = moments_call(wanted[0], half, shared, wd=weighted)[0]
+    pieces = [None, None, None, third]
     if dense:
-        held = first + mate
-        shares = lax.all_to_all(held, ("batch", "row"), split_axis=0, concat_axis=0, tiled=True)
+        mate = swap(third, "col")
+    for f in (1, 2, 0):
+        pieces[f] = moments_call(listed[f], group, shared, wd=weighted)[0]
+    if dense:
+        from_row = swap(pieces[1] + mate, "row")
+        mate = swap(pieces[2], "col")
+        held = (
+            pieces[0].astype(jnp.float32)
+            + mate.astype(jnp.float32)
+            + from_row.astype(jnp.float32)
+        ).astype(jnp.bfloat16)
+        shares = lax.all_to_all(held, "batch", split_axis=0, concat_axis=0, tiled=True)
         charges = jnp.sum(shares.astype(jnp.float32), axis=0)
         kernels = lax.dynamic_index_in_dim(green, row * sides + col, 0, keepdims=True)
         mine = apply_green(charges.reshape(1, width), kernels).reshape(1, lines, LANES)
@@ -469,10 +477,10 @@
             tiled=True,
         )
         beside = swap(own, "row")
-        beyond = lax.ppermute(own, plane, across)
+        beyond = swap(beside, "col")
         tables = [own, beside, swap(own, "col"), beyond]
     else:
-        moments = jnp.concatenate([first, other])
+        moments = jnp.concatenate(pieces)
         moments = moments.astype(jnp.float32).reshape(count, width)
         home = atoms // holding
         local_slot = atoms % holding
@@ -514,9 +522,15 @@
     ends = [basis_values, weights, basis_index]
     spread = functools.partial(field_call, size=group, shared=shared, keep=dense)
     field, *ours = spread((listed[0], listed[2]), tables=[tables[0], tables[2]])
-    load = spread((listed[1], listed[3]), tables=[tables[1], tables[3]], acc=field, ends=ends)
+    field, *half = spread((listed[1],), tables=[tables[1]], acc=field)
+    load = spread((listed[3],), tables=[tables[3]], acc=field, ends=ends)
     if dense:
-        ours, theirs = ours[0], load[4]
+        ours = ours[0]
+        theirs = jnp.where(
+            col == 0,
+            jnp.concatenate([half[0], load[4]]),
+            jnp.concatenate([load[4], half[0]]),
+        )
         potential = jnp.concatenate(
             [jnp.where(row == 0, ours, theirs), jnp.where(row == 0, theirs, ours)]
         ).reshape(holding, width)
@@ -528,7 +542,8 @@
             near.append(swap(plane_load, "batch", step))
         for line in near:
             far.append(swap(line, "batch"))
-        stages = [near[:1]] + [list(pair) for pair in zip(near[1:], far)] + [far[-1:]]
+        stages = [near[:1], far[:1]] + [near[1:2]] * (len(near) > 1)
+        stages += [list(pair) for pair in zip(near[2:], far[1:])] + [far[-1:]] * (len(near) > 1)
         total = None
         for order, lines in enumerate(stages):
             total = place_call(lines, piece, tile, total, final=lines is stages[-1])

time: 116 us -> 115 us (level)
  Pallas kernels: 41.7 us -> 49.5 us
  local copies, waits for them, and re-layouts: 8.31 us -> 2.13 us
  waiting for transfers between devices: 32 us -> 25.9 us
  starting transfers between devices: 19.8 us -> 22.2 us
  other arithmetic: 0.96 us -> 2.72 us
    ppermute x12 -> x15, starting transfers between devices: 9.65 us -> 16.2 us  [swap(): return lax.ppermute(value, axis, [(i, i ^ mask) for i in range(size)])]
    unnamed x38 -> x22, local copies, waits for them, and re-layouts: 6.97 us -> 0.77 us
    all_to_all x1, waiting for transfers between devices: 13 us -> 7.58 us  [on_device(): lax.all_to_all(held, 'batch', split_axis=0, concat_axis=0, tiled=True)]
    pallas_call x2 -> x4, Pallas kernels: 10 us -> 15.2 us  [moments_call(): pl.pallas_call(functools.partial(moments_kernel, group, count, fresh), ou...]
    ppermute x1 -> x0, waiting for transfers between devices: 3.29 us -> none  [on_device(): beyond = lax.ppermute(own, plane, across)]
    all_to_all x1, starting transfers between devices: 7.86 us -> 6.03 us  [on_device(): lax.all_to_all(held, 'batch', split_axis=0, concat_axis=0, tiled=True)]
    convert_element_type x0 -> x1, other arithmetic: none -> 1.68 us  [on_device(): held = (pieces[0].astype(jnp.float32) + mate.astype(jnp.float32) + from_r...]
    ppermute x1, waiting for transfers between devices: 0.01 us -> 1.53 us  [on_device(): lax.ppermute(load[3], plane, across)]
  transfers between devices with their start and end apart: 15 -> 17, of which waited for: 6 -> 8; matrix products, arithmetic and copies ran while one was open for 1% -> 2% of each run, Pallas kernels for 22% -> 32%
where the time goes in v2:
time: 115 us; the launch traced here: 114 us
  Pallas kernels  49.5 us (43%)
  waiting for transfers between devices  25.9 us (23%)
  starting transfers between devices  22.2 us (19%)
  blocking collectives  10.3 us (9%)
  other arithmetic  2.72 us (2%)
  local copies, waits for them, and re-layouts  2.13 us (2%)
    pallas_call x6, Pallas kernels, place_call(): pl.pallas_call(functools.partial(place_kernel, len(stacks), acc is not No...  21.1 us
    ppermute x15, waiting for transfers between devices, swap(): return lax.ppermute(value, axis, [(i, i ^ mask) for i in range(size)])  16.8 us
    ppermute x15, starting transfers between devices, swap(): return lax.ppermute(value, axis, [(i, i ^ mask) for i in range(size)])  16.2 us
    pallas_call x4, Pallas kernels, moments_call(): pl.pallas_call(functools.partial(moments_kernel, group, count, fresh), ou...  15.2 us
    pallas_call x3, Pallas kernels, field_call(): pl.pallas_call(functools.partial(field_kernel, groups, size, acc is not N...  13.1 us
    all_to_all x1, blocking collectives, on_device(): lax.all_to_all(jnp.broadcast_to(mine, (owners, lines, LANES)), 'batch', s...  10.3 us
    all_to_all x1, waiting for transfers between devices, on_device(): lax.all_to_all(held, 'batch', split_axis=0, concat_axis=0, tiled=True)  7.58 us
    all_to_all x1, starting transfers between devices, on_device(): lax.all_to_all(held, 'batch', split_axis=0, concat_axis=0, tiled=True)  6.03 us
  transfers between devices with their start and end apart: 17, of which 8 were waited for; matrix products, arithmetic and copies ran while one was open for 2% of the time, Pallas kernels for 32%

profile of v2, /device:TPU:0, one launch (start us, length us, event | category | flops | bytes accessed | tf_op | source)
XLA Modules:
  0.0 114.1 jit_solution(12776621670312967542)
XLA Ops:
  0.7 4.6 %moments.4 = (bf16[8,96,128]{2,1,0:T(8,128)(2,1)}, f32[3,2048]{1,0:T(4,128)}) custom-call(s32[32]{0:T(128)} %bitcast.23, f32[3,32]{1,0:T(4,128)} %refs_1_.13, s32[32]{0:T(128)} %refs_2_.13, f32[64]{0:T(128)} %refs_3_.13, f32[3,1,2048]{2,1,0:T(1,128)} %bitcast.16, bf16[1,192,2048]{2,1,0:T(8,128)(2,1)} %refs_7_.3, bf16[1,3,192,192]{3,2,1,0:T(8,128)(2,1)} %refs_6_.1, ...), custom_call_target="tpu_custom_call" | custom-call | flops 402653184 | bytes 1048576 | tf_op jit(solution)/shard_map/moments/pallas_call | solution.py:179
  5.8 3.5 %moments.6 = bf16[8,96,128]{2,1,0:T(8,128)(2,1)} custom-call(s32[32]{0:T(128)} %bitcast.24, f32[3,32]{1,0:T(4,128)} %refs_1_.13, s32[32]{0:T(128)} %refs_2_.13, f32[64]{0:T(128)} %refs_3_.13, f32[3,1,2048]{2,1,0:T(1,128)} %bitcast.17, f32[3,2048]{1,0:T(4,128)} %get-tuple-element.13.refs_5_), custom_call_target="tpu_custom_call" | custom-call | flops 402653184 | bytes 1048576 | tf_op jit(solution)/shard_map/moments/pallas_call | solution.py:179
  9.4 3.6 %moments.7 = bf16[8,96,128]{2,1,0:T(8,128)(2,1)} custom-call(s32[32]{0:T(128)} %bitcast.25, f32[3,32]{1,0:T(4,128)} %refs_1_.13, s32[32]{0:T(128)} %refs_2_.13, f32[64]{0:T(128)} %refs_3_.13, f32[3,1,2048]{2,1,0:T(1,128)} %bitcast.18, f32[3,2048]{1,0:T(4,128)} %get-tuple-element.13.refs_5_), custom_call_target="tpu_custom_call" | custom-call | flops 402653184 | bytes 1048576 | tf_op jit(solution)/shard_map/moments/pallas_call | solution.py:179
  14.0 3.0 %collective-permute-start.2 = (bf16[8,96,128]{2,1,0:T(8,128)(2,1)S(1)}, bf16[8,96,128]{2,1,0:T(8,128)(2,1)S(1)}, u32[]{:S(2)}, u32[]{:S(2)}) collective-permute-start(bf16[8,96,128]{2,1,0:T(8,128)(2,1)S(1)} %add.17), channel_id=1, source_target_pairs={{0,2},{2,0},{1,3},{3,1},{4,6},{6,4},{5,7},{7,5},{8,10},{10,8},{9,1... | collective-permute-start | bytes 589832 | tf_op jit(solution)/shard_map/ppermute | solution.py:418
  17.0 3.5 %moments.5 = bf16[8,96,128]{2,1,0:T(8,128)(2,1)} custom-call(s32[32]{0:T(128)} %bitcast.26, f32[3,32]{1,0:T(4,128)} %refs_1_.13, s32[32]{0:T(128)} %refs_2_.13, f32[64]{0:T(128)} %refs_3_.13, f32[3,1,2048]{2,1,0:T(1,128)} %bitcast.19, f32[3,2048]{1,0:T(4,128)} %get-tuple-element.13.refs_5_), custom_call_target="tpu_custom_call" | custom-call | flops 402653184 | bytes 1048576 | tf_op jit(solution)/shard_map/moments/pallas_call | solution.py:179
  22.1 1.7 %add_convert_fusion = bf16[8,96,128]{2,1,0:T(8,128)(2,1)} fusion(bf16[8,96,128]{2,1,0:T(8,128)(2,1)S(1)} %collective-permute-done.2, bf16[8,96,128]{2,1,0:T(8,128)(2,1)S(1)} %collective-permute-done, bf16[8,96,128]{2,1,0:T(8,128)(2,1)} %moments.5), kind=kLoop, calls=%fused_computation.3 | loop fusion | flops 589824 | bytes 786432 | tf_op jit(solution)/shard_map/convert_element_type | solution.py:467
  23.8 6.0 %all-to-all-start = ((bf16[8,96,128]{2,1,0:T(8,128)(2,1)}), bf16[8,96,128]{2,1,0:T(8,128)(2,1)S(1)}, u32[]{:S(2)}, u32[]{:S(2)}) async-start(bf16[8,96,128]{2,1,0:T(8,128)(2,1)} %add_convert_fusion), calls=%async_computation | async-start | bytes 393216 | tf_op jit(solution)/shard_map/all_to_all | solution.py:468
  30.0 7.6 %all-to-all-done = bf16[8,96,128]{2,1,0:T(8,128)(2,1)S(1)} async-done(((bf16[8,96,128]{2,1,0:T(8,128)(2,1)}), bf16[8,96,128]{2,1,0:T(8,128)(2,1)S(1)}, u32[]{:S(2)}, u32[]{:S(2)}) %all-to-all-start) | async-done | bytes 196640 | tf_op jit(solution)/shard_map/all_to_all | solution.py:468
  39.1 10.3 %all_to_all.10.refs_5_ = bf16[8,96,128]{2,1,0:T(8,128)(2,1)S(1)} all-to-all(bf16[8,96,128]{2,1,0:T(8,128)(2,1)S(1)} %broadcast_in_dim.8), channel_id=1, replica_groups=mesh['batch'=8,'row'=2,'col'=2] {'batch'}, dimensions={0} | all-to-all | bytes 393216 | tf_op jit(solution)/shard_map/all_to_all | solution.py:472
  50.9 4.1 %collective-permute-done.4.refs_5_ = bf16[8,96,128]{2,1,0:T(8,128)(2,1)S(1)} collective-permute-done((bf16[8,96,128]{2,1,0:T(8,128)(2,1)S(1)}, bf16[8,96,128]{2,1,0:T(8,128)(2,1)S(1)}, u32[]{:S(2)}, u32[]{:S(2)}) %collective-permute-start.4) | collective-permute-done | bytes 196640 | tf_op jit(solution)/shard_map/ppermute | solution.py:418
  55.1 5.5 %field.3 = (f32[24,2048]{1,0:T(8,128)S(1)}, bf16[2,96,128]{2,1,0:T(8,128)(2,1)S(1)}) custom-call(s32[32]{0:T(128)S(1)} %bitcast.27, f32[3,32]{1,0:T(4,128)S(1)} %copy-done.4, s32[32]{0:T(128)S(1)} %copy-done.7, f32[64]{0:T(128)S(1)} %copy-done.8, f32[3,1,2048]{2,1,0:T(1,128)S(1)} %bitcast.20, bf16[8,96,128]{2,1,0:T(8,128)(2,1)S(1)} %all_to_all.10.refs_5_, ...), custom_call_target="tpu_custom_call" | custom-call | flops 805306368 | bytes 2097152 | tf_op jit(solution)/shard_map/field/pallas_call | solution.py:307
  60.6 3.0 %field.4 = (f32[24,2048]{1,0:T(8,128)S(1)}, bf16[1,96,128]{2,1,0:T(8,128)(2,1)S(1)}) custom-call(s32[32]{0:T(128)S(1)} %bitcast.28, f32[3,32]{1,0:T(4,128)S(1)} %copy-done.4, s32[32]{0:T(128)S(1)} %copy-done.7, f32[64]{0:T(128)S(1)} %copy-done.8, f32[3,1,2048]{2,1,0:T(1,128)S(1)} %bitcast.21, bf16[8,96,128]{2,1,0:T(8,128)(2,1)S(1)} %collective-permute-done.4.refs_5_, ...), custom_call_target="tpu_custom_call" | custom-call | flops 402653184 | bytes 1048576 | tf_op jit(solution)/shard_map/field/pallas_call | solution.py:307
  63.6 4.6 %field.5 = (bf16[1,224,128]{2,1,0:T(8,128)(2,1)S(1)}, bf16[1,224,128]{2,1,0:T(8,128)(2,1)S(1)}, bf16[1,224,128]{2,1,0:T(8,128)(2,1)S(1)}, bf16[1,224,128]{2,1,0:T(8,128)(2,1)S(1)}, bf16[1,96,128]{2,1,0:T(8,128)(2,1)S(1)}) custom-call(s32[32]{0:T(128)S(1)} %bitcast.29, f32[3,32]{1,0:T(4,128)S(1)} %copy-done.4, s32[32]{0:T(128)S(1)} %copy-done.7, ...), custom_call_target="tpu_custom_call" | custom-call | flops 402653184 | bytes 1048576 | tf_op jit(solution)/shard_map/field/pallas_call | solution.py:307
  71.1 1.9 %collective-permute-done.7 = bf16[1,224,128]{2,1,0:T(8,128)(2,1)S(1)} collective-permute-done((bf16[1,224,128]{2,1,0:T(8,128)(2,1)S(1)}, bf16[1,224,128]{2,1,0:T(8,128)(2,1)S(1)}, u32[]{:S(2)}, u32[]{:S(2)}) %collective-permute-start.7) | collective-permute-done | bytes 57376 | tf_op jit(solution)/shard_map/ppermute | solution.py:418
  76.0 2.6 %place.6.refs_1_ = f32[3,768,768]{2,1,0:T(8,128)S(1)} custom-call(bf16[4,224,128]{2,1,0:T(8,128)(2,1)S(1)} %constant_dynamic-update-slice_fusion.refs_0_), custom_call_target="tpu_custom_call" | custom-call | flops 5435817984 | bytes 7077888 | tf_op jit(solution)/shard_map/place/pallas_call | solution.py:388
  79.8 2.0 %collective-permute-start.9 = (bf16[4,224,128]{2,1,0:T(8,128)(2,1)S(1)}, bf16[4,224,128]{2,1,0:T(8,128)(2,1)S(1)}, u32[]{:S(2)}, u32[]{:S(2)}) collective-permute-start(bf16[4,224,128]{2,1,0:T(8,128)(2,1)S(1)} %constant_dynamic-update-slice_fusion.refs_0_), channel_id=1, source_target_pairs={{0,24},{4,28},{8,16},{12,20},{16,8},{20,12},{24,0},{28,4},{1,25},{... | collective-permute-start | bytes 688136 | tf_op jit(solution)/shard_map/ppermute | solution.py:418
  82.8 2.4 %collective-permute-start.14 = (bf16[4,224,128]{2,1,0:T(8,128)(2,1)S(1)}, bf16[4,224,128]{2,1,0:T(8,128)(2,1)S(1)}, u32[]{:S(2)}, u32[]{:S(2)}) collective-permute-start(bf16[4,224,128]{2,1,0:T(8,128)(2,1)S(1)} %collective-permute-done.13.refs_0_), channel_id=1, source_target_pairs={{0,4},{4,0},{8,12},{12,8},{16,20},{20,16},{24,28},{28,24},{1,5},{5... | collective-permute-start | bytes 688136 | tf_op jit(solution)/shard_map/ppermute | solution.py:418
  85.2 2.9 %place.7.refs_1_ = f32[3,768,768]{2,1,0:T(8,128)S(1)} custom-call(bf16[4,224,128]{2,1,0:T(8,128)(2,1)S(1)} %collective-permute-done.15.refs_0_, f32[3,768,768]{2,1,0:T(8,128)S(1)} %place.6.refs_1_), custom_call_target="tpu_custom_call", output_to_operand_aliasing={{}: (1, {})} | custom-call | flops 5435817984 | bytes 7077888 | tf_op jit(solution)/shard_map/place/pallas_call | solution.py:388
  88.1 2.9 %place.8.refs_2_ = f32[3,768,768]{2,1,0:T(8,128)S(1)} custom-call(bf16[4,224,128]{2,1,0:T(8,128)(2,1)S(1)} %collective-permute-done.13.refs_0_, f32[3,768,768]{2,1,0:T(8,128)S(1)} %place.7.refs_1_), custom_call_target="tpu_custom_call", output_to_operand_aliasing={{}: (1, {})} | custom-call | flops 5435817984 | bytes 7077888 | tf_op jit(solution)/shard_map/place/pallas_call | solution.py:388
  91.0 6.0 %collective-permute-done.11.refs_0_ = bf16[4,224,128]{2,1,0:T(8,128)(2,1)S(1)} collective-permute-done((bf16[4,224,128]{2,1,0:T(8,128)(2,1)S(1)}, bf16[4,224,128]{2,1,0:T(8,128)(2,1)S(1)}, u32[]{:S(2)}, u32[]{:S(2)}) %collective-permute-start.11) | collective-permute-done | bytes 229408 | tf_op jit(solution)/shard_map/ppermute | solution.py:418
  99.1 4.4 %place.9.refs_2_ = f32[3,768,768]{2,1,0:T(8,128)S(1)} custom-call(bf16[4,224,128]{2,1,0:T(8,128)(2,1)S(1)} %collective-permute-done.11.refs_0_, bf16[4,224,128]{2,1,0:T(8,128)(2,1)S(1)} %collective-permute-done.14.refs_1_, f32[3,768,768]{2,1,0:T(8,128)S(1)} %place.8.refs_2_), custom_call_target="tpu_custom_call", output_to_operand_aliasing={{}: (2, {})} | custom-call | flops 10871635968 | bytes 7077888 | tf_op jit(solution)/shard_map/place/pallas_call | solution.py:388
  103.5 2.0 %collective-permute-done.12.refs_1_ = bf16[4,224,128]{2,1,0:T(8,128)(2,1)S(1)} collective-permute-done((bf16[4,224,128]{2,1,0:T(8,128)(2,1)S(1)}, bf16[4,224,128]{2,1,0:T(8,128)(2,1)S(1)}, u32[]{:S(2)}, u32[]{:S(2)}) %collective-permute-start.12) | collective-permute-done | bytes 229408 | tf_op jit(solution)/shard_map/ppermute | solution.py:418
  105.5 4.6 %place.10.refs_1_ = f32[3,768,768]{2,1,0:T(8,128)S(1)} custom-call(bf16[4,224,128]{2,1,0:T(8,128)(2,1)S(1)} %collective-permute-done.9.refs_0_, bf16[4,224,128]{2,1,0:T(8,128)(2,1)S(1)} %collective-permute-done.12.refs_1_, f32[3,768,768]{2,1,0:T(8,128)S(1)} %place.9.refs_2_), custom_call_target="tpu_custom_call", output_to_operand_aliasing={{}: (2, {})} | custom-call | flops 10871635968 | bytes 7077888 | tf_op jit(solution)/shard_map/place/pallas_call | solution.py:388
  110.1 3.8 %place.11 = bf16[3,768,768]{2,1,0:T(8,128)(2,1)} custom-call(bf16[4,224,128]{2,1,0:T(8,128)(2,1)S(1)} %collective-permute-done.10.refs_0_, f32[3,768,768]{2,1,0:T(8,128)S(1)} %place.10.refs_1_), custom_call_target="tpu_custom_call" | custom-call | flops 5435817984 | bytes 7077888 | tf_op jit(solution)/shard_map/place/pallas_call | solution.py:388
  (59 shorter events, 16.5 us)
Async XLA Ops:
  0.6 54.4 %copy-start.6 = (s32[1,32]{1,0:T(1,128)S(1)}, s32[1,32]{1,0:T(1,128)}, u32[]{:S(2)}) copy-start(s32[1,32]{1,0:T(1,128)} %param.14) | copy-start | bytes 388
  0.7 54.4 %copy-start.2 = (f32[1,3,2048]{2,0,1:T(1,128)S(1)}, f32[1,3,2048]{2,0,1:T(1,128)}, u32[]{:S(2)}) copy-start(f32[1,3,2048]{2,0,1:T(1,128)} %param.12) | copy-start | bytes 73732
  0.7 54.4 %copy-start.4 = (f32[3,32]{1,0:T(4,128)S(1)}, f32[3,32]{1,0:T(4,128)}, u32[]{:S(2)}) copy-start(f32[3,32]{1,0:T(4,128)} %refs_1_.13) | copy-start | bytes 1156
  0.7 54.4 %copy-start.7 = (s32[32]{0:T(128)S(1)}, s32[32]{0:T(128)}, u32[]{:S(2)}) copy-start(s32[32]{0:T(128)} %refs_2_.13) | copy-start | bytes 388
  0.7 54.4 %copy-start.8 = (f32[64]{0:T(128)S(1)}, f32[64]{0:T(128)}, u32[]{:S(2)}) copy-start(f32[64]{0:T(128)} %refs_3_.13) | copy-start | bytes 772
  5.3 7.7 %collective-permute-start.1 = (bf16[8,96,128]{2,1,0:T(8,128)(2,1)}, bf16[8,96,128]{2,1,0:T(8,128)(2,1)S(1)}, u32[]{:S(2)}, u32[]{:S(2)}) collective-permute-start(bf16[8,96,128]{2,1,0:T(8,128)(2,1)} %get-tuple-element.14), channel_id=1, source_target_pairs={{0,1},{1,0},{2,3},{3,2},{4,5},{5,4},{6,7},{7,6},{8,9},{9,8},{10,11... | collective-permute-start | bytes 589832 | tf_op jit(solution)/shard_map/ppermute | solution.py:418
  9.3 54.3 %copy-start.3 = (f32[1,2048]{1,0:T(1,128)S(1)}, f32[1,2048]{1,0:T(1,128)}, u32[]{:S(2)}) copy-start(f32[1,2048]{1,0:T(1,128)} %refs_8_.1) | copy-start | bytes 24580
  9.3 54.3 %copy-start.5 = (s32[1,192]{1,0:T(1,128)S(1)}, s32[1,192]{1,0:T(1,128)}, u32[]{:S(2)}) copy-start(s32[1,192]{1,0:T(1,128)} %refs_9_.1) | copy-start | bytes 2308
  9.3 11.1 %collective-permute-start = (bf16[8,96,128]{2,1,0:T(8,128)(2,1)}, bf16[8,96,128]{2,1,0:T(8,128)(2,1)S(1)}, u32[]{:S(2)}, u32[]{:S(2)}) collective-permute-start(bf16[8,96,128]{2,1,0:T(8,128)(2,1)} %moments.6), channel_id=1, source_target_pairs={{0,1},{1,0},{2,3},{3,2},{4,5},{5,4},{6,7},{7,6},{8,9},{9,8},{10,11... | collective-permute-start | bytes 589832 | tf_op jit(solution)/shard_map/ppermute | solution.py:418
  14.0 8.1 %collective-permute-start.2 = (bf16[8,96,128]{2,1,0:T(8,128)(2,1)S(1)}, bf16[8,96,128]{2,1,0:T(8,128)(2,1)S(1)}, u32[]{:S(2)}, u32[]{:S(2)}) collective-permute-start(bf16[8,96,128]{2,1,0:T(8,128)(2,1)S(1)} %add.17), channel_id=1, source_target_pairs={{0,2},{2,0},{1,3},{3,1},{4,6},{6,4},{5,7},{7,5},{8,10},{10,8},{9,1... | collective-permute-start | bytes 589832 | tf_op jit(solution)/shard_map/ppermute | solution.py:418
  23.8 13.8 %all-to-all-start = ((bf16[8,96,128]{2,1,0:T(8,128)(2,1)}), bf16[8,96,128]{2,1,0:T(8,128)(2,1)S(1)}, u32[]{:S(2)}, u32[]{:S(2)}) async-start(bf16[8,96,128]{2,1,0:T(8,128)(2,1)} %add_convert_fusion), calls=%async_computation | async-start | bytes 393216 | tf_op jit(solution)/shard_map/all_to_all | solution.py:468
  49.4 5.7 %collective-permute-start.4 = (bf16[8,96,128]{2,1,0:T(8,128)(2,1)S(1)}, bf16[8,96,128]{2,1,0:T(8,128)(2,1)S(1)}, u32[]{:S(2)}, u32[]{:S(2)}) collective-permute-start(bf16[8,96,128]{2,1,0:T(8,128)(2,1)S(1)} %all_to_all.10.refs_5_), channel_id=1, source_target_pairs={{0,2},{2,0},{1,3},{3,1},{4,6},{6,4},{5,7},{7,5},{8,10},{10,8},{9,1... | collective-permute-start | bytes 589832 | tf_op jit(solution)/shard_map/ppermute | solution.py:418
  50.9 4.2 %collective-permute-start.3 = (bf16[8,96,128]{2,1,0:T(8,128)(2,1)S(1)}, bf16[8,96,128]{2,1,0:T(8,128)(2,1)S(1)}, u32[]{:S(2)}, u32[]{:S(2)}) collective-permute-start(bf16[8,96,128]{2,1,0:T(8,128)(2,1)S(1)} %all_to_all.10.refs_5_), channel_id=1, source_target_pairs={{0,1},{1,0},{2,3},{3,2},{4,5},{5,4},{6,7},{7,6},{8,9},{9,8},{10,11... | collective-permute-start | bytes 589832 | tf_op jit(solution)/shard_map/ppermute | solution.py:418
  55.0 8.5 %collective-permute-start.5 = (bf16[8,96,128]{2,1,0:T(8,128)(2,1)S(1)}, bf16[8,96,128]{2,1,0:T(8,128)(2,1)S(1)}, u32[]{:S(2)}, u32[]{:S(2)}) collective-permute-start(bf16[8,96,128]{2,1,0:T(8,128)(2,1)S(1)} %collective-permute-done.4.refs_5_), channel_id=1, source_target_pairs={{0,1},{1,0},{2,3},{3,2},{4,5},{5,4},{6,7},{7,6},{8,9},{9,8},{10,11... | collective-permute-start | bytes 589832 | tf_op jit(solution)/shard_map/ppermute | solution.py:418
  68.3 2.8 %collective-permute-start.6 = (bf16[1,224,128]{2,1,0:T(8,128)(2,1)S(1)}, bf16[1,224,128]{2,1,0:T(8,128)(2,1)S(1)}, u32[]{:S(2)}, u32[]{:S(2)}) collective-permute-start(bf16[1,224,128]{2,1,0:T(8,128)(2,1)S(1)} %get-tuple-element.21), channel_id=1, source_target_pairs={{0,1},{1,0},{2,3},{3,2},{4,5},{5,4},{6,7},{7,6},{8,9},{9,8},{10,11... | collective-permute-start | bytes 172040 | tf_op jit(solution)/shard_map/ppermute | solution.py:418
  68.8 4.2 %collective-permute-start.7 = (bf16[1,224,128]{2,1,0:T(8,128)(2,1)S(1)}, bf16[1,224,128]{2,1,0:T(8,128)(2,1)S(1)}, u32[]{:S(2)}, u32[]{:S(2)}) collective-permute-start(bf16[1,224,128]{2,1,0:T(8,128)(2,1)S(1)} %get-tuple-element.22), channel_id=1, source_target_pairs={{0,2},{2,0},{1,3},{3,1},{4,6},{6,4},{5,7},{7,5},{8,10},{10,8},{9,1... | collective-permute-start | bytes 172040 | tf_op jit(solution)/shard_map/ppermute | solution.py:418
  70.3 4.2 %collective-permute-start.8 = (bf16[1,224,128]{2,1,0:T(8,128)(2,1)S(1)}, bf16[1,224,128]{2,1,0:T(8,128)(2,1)S(1)}, u32[]{:S(2)}, u32[]{:S(2)}) collective-permute-start(bf16[1,224,128]{2,1,0:T(8,128)(2,1)S(1)} %get-tuple-element.23), channel_id=1, source_target_pairs={{0,3},{1,2},{2,1},{3,0},{4,7},{5,6},{6,5},{7,4},{8,11},{9,10},{10,... | collective-permute-start | bytes 172040 | tf_op jit(solution)/shard_map/ppermute | solution.py:537
  74.6 10.7 %collective-permute-start.15 = (bf16[4,224,128]{2,1,0:T(8,128)(2,1)S(1)}, bf16[4,224,128]{2,1,0:T(8,128)(2,1)S(1)}, u32[]{:S(2)}, u32[]{:S(2)}) collective-permute-start(bf16[4,224,128]{2,1,0:T(8,128)(2,1)S(1)} %constant_dynamic-update-slice_fusion.refs_0_), channel_id=1, source_target_pairs={{0,4},{4,0},{8,12},{12,8},{16,20},{20,16},{24,28},{28,24},{1,5},{5... | collective-permute-start | bytes 688136 | tf_op jit(solution)/shard_map/ppermute | solution.py:418
  74.7 8.2 %collective-permute-start.13 = (bf16[4,224,128]{2,1,0:T(8,128)(2,1)S(1)}, bf16[4,224,128]{2,1,0:T(8,128)(2,1)S(1)}, u32[]{:S(2)}, u32[]{:S(2)}) collective-permute-start(bf16[4,224,128]{2,1,0:T(8,128)(2,1)S(1)} %constant_dynamic-update-slice_fusion.refs_0_), channel_id=1, source_target_pairs={{0,8},{4,12},{8,0},{12,4},{16,24},{20,28},{24,16},{28,20},{1,9},{5... | collective-permute-start | bytes 688136 | tf_op jit(solution)/shard_map/ppermute | solution.py:418
  78.6 18.4 %collective-permute-start.11 = (bf16[4,224,128]{2,1,0:T(8,128)(2,1)S(1)}, bf16[4,224,128]{2,1,0:T(8,128)(2,1)S(1)}, u32[]{:S(2)}, u32[]{:S(2)}) collective-permute-start(bf16[4,224,128]{2,1,0:T(8,128)(2,1)S(1)} %constant_dynamic-update-slice_fusion.refs_0_), channel_id=1, source_target_pairs={{0,16},{4,20},{8,24},{12,28},{16,0},{20,4},{24,8},{28,12},{1,17},{... | collective-permute-start | bytes 688136 | tf_op jit(solution)/shard_map/ppermute | solution.py:418
  79.8 18.7 %collective-permute-start.9 = (bf16[4,224,128]{2,1,0:T(8,128)(2,1)S(1)}, bf16[4,224,128]{2,1,0:T(8,128)(2,1)S(1)}, u32[]{:S(2)}, u32[]{:S(2)}) collective-permute-start(bf16[4,224,128]{2,1,0:T(8,128)(2,1)S(1)} %constant_dynamic-update-slice_fusion.refs_0_), channel_id=1, source_target_pairs={{0,24},{4,28},{8,16},{12,20},{16,8},{20,12},{24,0},{28,4},{1,25},{... | collective-permute-start | bytes 688136 | tf_op jit(solution)/shard_map/ppermute | solution.py:418
  82.8 16.2 %collective-permute-start.14 = (bf16[4,224,128]{2,1,0:T(8,128)(2,1)S(1)}, bf16[4,224,128]{2,1,0:T(8,128)(2,1)S(1)}, u32[]{:S(2)}, u32[]{:S(2)}) collective-permute-start(bf16[4,224,128]{2,1,0:T(8,128)(2,1)S(1)} %collective-permute-done.13.refs_0_), channel_id=1, source_target_pairs={{0,4},{4,0},{8,12},{12,8},{16,20},{20,16},{24,28},{28,24},{1,5},{5... | collective-permute-start | bytes 688136 | tf_op jit(solution)/shard_map/ppermute | solution.py:418
  97.0 8.5 %collective-permute-start.12 = (bf16[4,224,128]{2,1,0:T(8,128)(2,1)S(1)}, bf16[4,224,128]{2,1,0:T(8,128)(2,1)S(1)}, u32[]{:S(2)}, u32[]{:S(2)}) collective-permute-start(bf16[4,224,128]{2,1,0:T(8,128)(2,1)S(1)} %collective-permute-done.11.refs_0_), channel_id=1, source_target_pairs={{0,4},{4,0},{8,12},{12,8},{16,20},{20,16},{24,28},{28,24},{1,5},{5... | collective-permute-start | bytes 688136 | tf_op jit(solution)/shard_map/ppermute | solution.py:418
  98.5 11.6 %collective-permute-start.10 = (bf16[4,224,128]{2,1,0:T(8,128)(2,1)S(1)}, bf16[4,224,128]{2,1,0:T(8,128)(2,1)S(1)}, u32[]{:S(2)}, u32[]{:S(2)}) collective-permute-start(bf16[4,224,128]{2,1,0:T(8,128)(2,1)S(1)} %collective-permute-done.9.refs_0_), channel_id=1, source_target_pairs={{0,4},{4,0},{8,12},{12,8},{16,20},{20,16},{24,28},{28,24},{1,5},{5... | collective-permute-start | bytes 688136 | tf_op jit(solution)/shard_map/ppermute | solution.py:418
  (2 other events, 83.5 us)
